TPU v7x, 128 devices: a whole 4x4x4 slice. The times are simulated.
128 devices in a mesh: req: 32 (over z, y, x_lo), exp: 4 (over x_hi, core).
Axes of the slice: x: 4 (x_hi: 2, x_lo: 2; x = x_hi * 2 + x_lo), y: 4, z: 4, core: 2. Of those that a mesh axis runs over, the one named last changes fastest.
Arguments:
- hidden_in: bfloat16 [8192, 2048], P(('req', 'exp')), may hold values from -6 to 6
- query_in: bfloat16 [8192, 2048], P('req', 'exp'), may hold values from -6 to 6
- key_in: bfloat16 [8192, 2048], P('req', 'exp'), may hold values from -6 to 6
- value_in: bfloat16 [8192, 2048], P('req', 'exp'), may hold values from -24 to 24
- query_gain: float32 [128], replicated, may hold values from 0.5 to 2.5
- key_gain: float32 [128], replicated, may hold values from 0.5 to 2.5
- cache_keys: bfloat16 [64, 32, 2048], P('req', None, 'exp'), may hold values from -400 to 400
- cache_values: bfloat16 [64, 32, 2048], P('req', None, 'exp'), may hold values from -24 to 24
- cache_block: int32 [128], replicated, may hold values from -1 to 63, as said below
- request_lengths: int32 [32, 4], P('req'), may hold values from 1 to 128, 256 in all within a row
- out_proj: bfloat16 [2048, 2048], P('exp'), may hold values from -0.125 to 0.125
- norm_gain: float32 [2048], replicated, may hold values from 0.25 to 1.75
- expert_ids: int32 [8192, 8], P(('req', 'exp')), may hold values from 0 to 63, all different within a row; in each aligned block of 64 rows (0 to 63, 64 to 127, ...) at most 10 rows name the same one
- gate_values: float32 [8192, 8], P(('req', 'exp')), may hold values from 0.4 to 1.6
- old_slots: int32 [64], replicated, may hold values from 0 to 63, each once
- new_replicas: int32 [32], replicated, may hold values from 0 to 63
- slot_weights: bfloat16 [64, 3, 2048, 1024], P('req', None, None, 'exp'), may hold values from -0.125 to 0.125
Outputs:
- layer_out: bfloat16 [8192, 2048], P(('req', 'exp'))
- replica_weights: bfloat16 [32, 3, 2048, 1024], P('req', None, None, 'exp')
Inputs may be any that keep to these rules, and one draw needn't show every extreme that they name: `cache_block`: each index of req has exactly 2 of its 4 requests with a block; every block serves exactly one request. `expert_ids`: in each aligned block of 64 rows (the rows of one device) no expert is named by more than 10 rows, a bound that some block reaches; the 8 experts of a row differ. `old_slots`: every expert is in exactly one slot. `request_lengths`: the lengths of each index of req sum to 256.
All inputs are finite; a program needn't handle non-finite values.
Results may differ from a plain program's by a relative error of at most 0.025.
Values may be sent and summed in bfloat16 or wider, within the bound.
A program may use at most 128 MiB of HBM per device.

v0:
```python
import functools
import math

import jax
import jax.numpy as jnp
from jax import lax
from jax.experimental import pallas as pl
from jax.experimental.pallas import tpu as pltpu
from jax.sharding import PartitionSpec as P

MESH = pl.DeviceIdType.MESH


def cache_kernel(n, need_ref, both_ref, out_ref, stage, send_buf, land, sems):
    me = lax.axis_index("req")
    ex = lax.axis_index("exp")
    barrier = pltpu.get_barrier_semaphore()

    def greet(k, carry):
        peer = lax.rem(me + k, n)
        pl.semaphore_signal(barrier, inc=1, device_id=(peer, ex), device_id_type=MESH)
        return carry

    lax.fori_loop(1, n, greet, 0)
    pl.semaphore_wait(barrier, n - 1)

    def first_copy(k, peer):
        return pltpu.make_async_remote_copy(
            src_ref=both_ref.at[peer],
            dst_ref=stage.at[me],
            send_sem=sems.at[0, k],
            recv_sem=sems.at[1, k],
            device_id=(peer, ex),
            device_id_type=MESH,
        )

    def second_copy(k, peer):
        return pltpu.make_async_remote_copy(
            src_ref=send_buf.at[k],
            dst_ref=land.at[me],
            send_sem=sems.at[2, k],
            recv_sem=sems.at[3, k],
            device_id=(peer, ex),
            device_id_type=MESH,
        )

    def send_first(k, carry):
        first_copy(k, lax.rem(me + k, n)).start()
        return carry

    lax.fori_loop(1, n, send_first, 0)
    stage[me] = both_ref[me]

    def wait_first(k, carry):
        source = lax.rem(me + n - k, n)
        pltpu.make_async_remote_copy(
            src_ref=both_ref.at[me],
            dst_ref=stage.at[source],
            send_sem=sems.at[0, k],
            recv_sem=sems.at[1, k],
            device_id=(source, ex),
            device_id_type=MESH,
        ).wait_recv()
        return carry

    lax.fori_loop(1, n, wait_first, 0)
    rows = lax.broadcasted_iota(jnp.int32, both_ref.shape[1:], 0)

    def pieces_for(dest):
        picked = []
        for c in range(2):
            block = need_ref[dest * 2 + c]
            slab = stage[block // 2].astype(jnp.float32)
            one = jnp.where(block % 2 == 0, slab[0:1], slab[1:2])
            picked.append(jnp.broadcast_to(one, slab.shape))
        return jnp.where(rows == 0, picked[0], picked[1]).astype(land.dtype)

    def send_second(k, carry):
        dest = lax.rem(me + k, n)
        send_buf[k] = pieces_for(dest)
        second_copy(k, dest).start()
        return carry

    lax.fori_loop(1, n, send_second, 0)
    land[me] = pieces_for(me)

    def wait_second(k, carry):
        source = lax.rem(me + n - k, n)
        pltpu.make_async_remote_copy(
            src_ref=send_buf.at[k],
            dst_ref=land.at[source],
            send_sem=sems.at[2, k],
            recv_sem=sems.at[3, k],
            device_id=(source, ex),
            device_id_type=MESH,
        ).wait_recv()
        first_copy(k, lax.rem(me + k, n)).wait_send()
        second_copy(k, lax.rem(me + k, n)).wait_send()
        return carry

    lax.fori_loop(1, n, wait_second, 0)
    out_ref[...] = land[...]


def exchange_cache(both_t, need_flat, n):
    shape = both_t.shape
    return pl.pallas_call(
        functools.partial(cache_kernel, n),
        out_shape=jax.ShapeDtypeStruct(shape, both_t.dtype),
        in_specs=[
            pl.BlockSpec(memory_space=pltpu.SMEM),
            pl.BlockSpec(memory_space=pltpu.VMEM),
        ],
        out_specs=pl.BlockSpec(memory_space=pltpu.VMEM),
        scratch_shapes=[
            pltpu.VMEM(shape, both_t.dtype),
            pltpu.VMEM(shape, both_t.dtype),
            pltpu.VMEM(shape, both_t.dtype),
            pltpu.SemaphoreType.DMA((4, n)),
        ],
        compiler_params=pltpu.CompilerParams(collective_id=0, has_side_effects=True),
    )(need_flat, both_t)


def prepare(values, gain, position):
    vector = values.astype(jnp.float32)
    scaled = vector * lax.rsqrt(jnp.mean(vector * vector, axis=-1, keepdims=True) + 1e-06) * gain
    half_size = scaled.shape[-1] // 2
    frequency = 10000.0 ** (-(jnp.arange(half_size, dtype=jnp.float32) * 2.0 / scaled.shape[-1]))
    angles = position[:, None] * frequency[None, :]
    cosine = jnp.cos(angles)[:, None, :]
    sine_part = jnp.sin(angles)[:, None, :]
    lower_half = scaled[..., :half_size]
    upper_half = scaled[..., half_size:]
    rotated = jnp.concatenate(
        [
            lower_half * cosine - upper_half * sine_part,
            upper_half * cosine + lower_half * sine_part,
        ],
        axis=-1,
    )
    return rotated.astype(jnp.bfloat16)


def compact(block_rows, slots_wanted):
    live = block_rows >= 0
    ranks = jnp.cumsum(live.astype(jnp.int32), axis=1) - 1
    request_idx = jnp.arange(block_rows.shape[1], dtype=jnp.int32)[None, :]
    chosen_blocks = []
    chosen_requests = []
    for slot_num in range(slots_wanted):
        picked = live & (ranks == slot_num)
        chosen_blocks.append(jnp.sum(jnp.where(picked, block_rows, 0), axis=1))
        chosen_requests.append(jnp.sum(jnp.where(picked, request_idx, 0), axis=1))
    return (jnp.stack(chosen_blocks, axis=1), jnp.stack(chosen_requests, axis=1))


def body(
    hidden_in,
    query_in,
    key_in,
    value_in,
    query_gain,
    key_gain,
    cache_keys,
    cache_values,
    cache_block,
    request_lengths,
    out_proj,
    norm_gain,
    expert_ids,
    gate_values,
    old_slots,
    new_replicas,
    slot_weights,
):
    req_count = lax.axis_size("req")
    exp_count = lax.axis_size("exp")
    group_idx = lax.axis_index("req")
    tok_grp, width_q = query_in.shape
    tok_dev, model_width = hidden_in.shape
    head_size = query_gain.shape[0]
    head_count = width_q // head_size
    cache_dev = cache_keys.shape[0]
    pre_len = cache_keys.shape[1]
    req_grp = request_lengths.shape[1]
    lengths = request_lengths[0]
    req_ends = jnp.cumsum(lengths)
    starts = req_ends - lengths
    places = jnp.arange(tok_grp, dtype=jnp.int32)
    member = (places[:, None] >= starts[None, :]) & (places[:, None] < req_ends[None, :])
    request_idx = jnp.arange(req_grp, dtype=jnp.int32)
    segment = jnp.sum(jnp.where(member, request_idx[None, :], 0), axis=1)
    offset = places - jnp.sum(jnp.where(member, starts[None, :], 0), axis=1)
    block_rows = cache_block.reshape(req_count, req_grp)
    my_blocks = lax.dynamic_index_in_dim(block_rows, group_idx, 0, keepdims=False)
    has_cache = my_blocks >= 0
    token_cached = jnp.sum(jnp.where(member & has_cache[None, :], 1, 0), axis=1) > 0
    position = (offset + jnp.where(token_cached, pre_len, 0)).astype(jnp.float32)
    need_blocks, need_requests = compact(block_rows, cache_dev)
    my_requests = lax.dynamic_index_in_dim(need_requests, group_idx, 0, keepdims=False)
    key_width = cache_keys.shape[2]
    both = jnp.concatenate([cache_keys, cache_values], axis=-1)
    both_t = both.transpose(1, 0, 2)
    gathered = exchange_cache(both_t, need_blocks.reshape(-1).astype(jnp.int32), req_count)
    gathered = gathered.transpose(1, 0, 2)
    slot_weights, gathered = lax.optimization_barrier((slot_weights, gathered))
    far_keys = gathered[..., :key_width]
    far_values = gathered[..., key_width:]
    query_n = prepare(query_in.reshape(tok_grp, head_count, head_size), query_gain, position)
    key_n = prepare(key_in.reshape(tok_grp, head_count, head_size), key_gain, position)
    keyset = jnp.concatenate(
        [key_n, far_keys.reshape(cache_dev * pre_len, head_count, head_size)], axis=0
    )
    valueset = jnp.concatenate(
        [
            value_in.reshape(tok_grp, head_count, head_size),
            far_values.reshape(cache_dev * pre_len, head_count, head_size),
        ],
        axis=0,
    )
    key_request = jnp.concatenate([segment, jnp.repeat(my_requests, pre_len)])
    allowed = segment[:, None] == key_request[None, :]
    scores = jnp.einsum("qhd,khd->hqk", query_n, keyset, preferred_element_type=jnp.float32) * (
        1.0 / math.sqrt(head_size)
    )
    scores = jnp.where(allowed[None], scores, -1e30)
    peak = jnp.max(scores, axis=-1, keepdims=True)
    expos = jnp.exp(scores - peak)
    weights = (expos / jnp.sum(expos, axis=-1, keepdims=True)).astype(jnp.bfloat16)
    attended = jnp.einsum("hqk,khd->qhd", weights, valueset, preferred_element_type=jnp.float32)
    attended = attended.astype(jnp.bfloat16).reshape(tok_grp, width_q)
    attn_out = lax.psum_scatter(
        jnp.dot(attended, out_proj, preferred_element_type=jnp.float32),
        "exp",
        scatter_dimension=0,
        tiled=True,
    )
    residual = hidden_in.astype(jnp.float32) + attn_out
    normed = (
        residual
        * lax.rsqrt(jnp.mean(residual * residual, axis=-1, keepdims=True) + 1e-06)
        * norm_gain
    ).astype(jnp.bfloat16)
    topk_count = expert_ids.shape[1]
    slot_total = old_slots.shape[0]
    slots_here = slot_weights.shape[0]
    capacity = max(2, tok_dev * topk_count * 5 // (4 * slot_total))
    slot_range = jnp.arange(slot_total, dtype=jnp.int32)
    slot_of = jnp.sum(
        jnp.where(old_slots[None, :] == slot_range[:, None], slot_range[None, :], 0), axis=1
    )
    flat_ids = expert_ids.reshape(-1)
    onehot = flat_ids[:, None] == slot_range[None, :]
    row_slot = jnp.sum(jnp.where(onehot, slot_of[None, :], 0), axis=1)
    before = jnp.cumsum(onehot.astype(jnp.int32), axis=0) - onehot.astype(jnp.int32)
    row_rank = jnp.sum(jnp.where(onehot, before, 0), axis=1)
    target = row_slot * capacity + row_rank
    exp_idx = lax.axis_index("exp")
    pair_bit = exp_idx % 2
    pair_count = exp_count // 2
    own_part = lax.dynamic_index_in_dim(slot_weights, pair_bit, 0, keepdims=False)
    give_part = lax.dynamic_index_in_dim(slot_weights, 1 - pair_bit, 0, keepdims=False)
    swap = [(e, e ^ 1) for e in range(exp_count)]
    got_part = lax.ppermute(give_part, "exp", perm=swap)
    lanes = 128
    tile_rows = capacity * model_width // lanes

    def as_tiles(rows):
        return rows.reshape(req_count * exp_count, tile_rows, lanes)

    def as_rows(tiles):
        return tiles.reshape(req_count * exp_count * capacity, model_width)

    tile_high = model_width // lanes
    normed_tiles = normed.reshape(tok_dev, tile_high, lanes)
    row_token = jnp.arange(tok_dev * topk_count, dtype=jnp.int32) // topk_count
    source_token = jnp.zeros((slot_total * capacity,), jnp.int32).at[target].set(row_token)
    filled = jnp.zeros((slot_total * capacity,), jnp.bool_).at[target].set(True)
    outbox = jnp.where(filled[:, None, None], normed_tiles[source_token], jnp.bfloat16(0))
    outbox = outbox.reshape(req_count, 1, slots_here * tile_rows, lanes)
    copies = jnp.broadcast_to(outbox, (req_count, pair_count, slots_here * tile_rows, lanes))
    copies = copies.reshape(req_count * exp_count, tile_rows, lanes)
    inbox = lax.all_to_all(copies, ("req", "exp"), split_axis=0, concat_axis=0, tiled=True)
    in_rows = as_rows(inbox)
    halves = []
    for part in (own_part, got_part):
        gate_act = jnp.dot(in_rows, part[0], preferred_element_type=jnp.float32)
        up_act = jnp.dot(in_rows, part[1], preferred_element_type=jnp.float32)
        hidden = (jax.nn.silu(gate_act) * up_act).astype(jnp.bfloat16)
        piece = lax.dot_general(
            hidden, part[2], (((1,), (1,)), ((), ())), preferred_element_type=jnp.float32
        )
        halves.append(piece.astype(jnp.bfloat16).astype(jnp.float32))
    partial_value = as_tiles((halves[0] + halves[1]).astype(jnp.bfloat16))
    returned = lax.all_to_all(
        partial_value, ("req", "exp"), split_axis=0, concat_axis=0, tiled=True
    ).reshape(req_count * exp_count * capacity, tile_high, lanes)
    dest_req = row_slot // slots_here
    dest_pos = row_slot % slots_here
    result_rows = None
    for pair_num in range(pair_count):
        where_from = (dest_req * exp_count + pair_num * slots_here + dest_pos) * capacity + row_rank
        one = jnp.take(returned, where_from, axis=0).astype(jnp.float32)
        result_rows = one if result_rows is None else result_rows + one
    mixture = jnp.sum(
        result_rows.reshape(tok_dev, topk_count, tile_high, lanes)
        * gate_values[:, :, None, None],
        axis=1,
    )
    residual_tiles = residual.reshape(tok_dev, tile_high, lanes)
    layer_out = (residual_tiles + mixture).astype(jnp.bfloat16).reshape(tok_dev, model_width)
    spread_slots = lax.all_to_all(slot_weights, "req", split_axis=2, concat_axis=0, tiled=True)
    replica_onehot = new_replicas[:, None] == slot_range[None, :]
    source_slot = jnp.sum(jnp.where(replica_onehot, slot_of[None, :], 0), axis=1)
    chosen_pieces = jnp.take(spread_slots, source_slot, axis=0)
    replica_weights = lax.all_to_all(chosen_pieces, "req", split_axis=0, concat_axis=2, tiled=True)
    return (layer_out, replica_weights)


def solution(mesh):
    in_specs = (
        P(("req", "exp"), None),
        P("req", "exp"),
        P("req", "exp"),
        P("req", "exp"),
        P(),
        P(),
        P("req", None, "exp"),
        P("req", None, "exp"),
        P(),
        P("req", None),
        P("exp", None),
        P(),
        P(("req", "exp"), None),
        P(("req", "exp"), None),
        P(),
        P(),
        P("req", None, None, "exp"),
    )
    out_specs = (P(("req", "exp"), None), P("req", None, None, "exp"))
    return jax.shard_map(body, mesh=mesh, in_specs=in_specs, out_specs=out_specs, check_vma=False)
```

profile of v0, /device:TPU:1, one launch (start us, length us, event | category | flops | bytes accessed | tf_op | source)
XLA Modules:
  0.0 400.9 jit_solution(15833814509978396892)
XLA Ops:
  11.8 20.2 %shard_map.176 = bf16[32,2,1024]{2,1,0:T(2,128)(2,1)} custom-call(s32[64]{0:T(128)} %reshape.277.need_ref, bf16[32,2,1024]{2,1,0:T(2,128)(2,1)} %maximum_bitcast_fusion.both_ref), custom_call_target="tpu_custom_call" | custom-call | tf_op jit(solution)/shard_map/pallas_call | solution.py:107
  31.9 10.5 %copy.105 = bf16[2,3,2048,256]{3,1,0,2:T(4,128)(2,1)} copy(bf16[2,3,2048,256]{3,2,1,0:T(8,128)(2,1)} %param.35) | data formatting | bytes 12582912 | tf_op jit(solution)/shard_map/optimization_barrier | solution.py:207
  42.4 5.1 %all-to-all-start.2 = ((bf16[2,3,2048,256]{3,1,0,2:T(4,128)(2,1)}), bf16[2,3,2048,256]{3,1,0,2:T(4,128)(2,1)}, u32[]{:S(2)}, u32[]{:S(2)}) async-start(bf16[2,3,2048,256]{3,1,0,2:T(4,128)(2,1)} %copy.105), calls=%async_computation.3 | async-start | bytes 16777216 | tf_op jit(solution)/shard_map/all_to_all | solution.py:313
  69.6 45.9 %reduce-scatter.2.cloned.1.call-done = f32[64,2048]{1,0:T(8,128)} async-done(((f32[256,2048]{1,0:T(8,128)}), f32[64,2048]{1,0:T(8,128)}) %reduce-scatter.2.cloned.1.call-update) | async-done | bytes 524304 | tf_op jit(solution)/shard_map/reduce_scatter | solution.py:233
  121.3 5.4 %bitcast_select_fusion = bf16[32,320,128]{2,1,0:T(8,128)(2,1)} fusion(pred[32,320]{1,0:T(8,128)(4,1)S(1)} %copy.103, bf16[32,320,128]{2,1,0:T(8,128)(2,1)} %bitcast.111), kind=kLoop, calls=%fused_computation.15 | loop fusion | flops 1310720 | bytes 5253120 | tf_op jit(solution)/shard_map/jit(_where)/select_n | solution.py:280
  126.7 36.0 %all-to-all-done.2 = bf16[2,3,2048,256]{3,1,0,2:T(4,128)(2,1)} async-done(((bf16[2,3,2048,256]{3,1,0,2:T(4,128)(2,1)}), bf16[2,3,2048,256]{3,1,0,2:T(4,128)(2,1)}, u32[]{:S(2)}, u32[]{:S(2)}) %all-to-all-start.2) | async-done | bytes 6291488 | tf_op jit(solution)/shard_map/all_to_all | solution.py:313
  162.6 5.5 %broadcast_in_dim.211 = bf16[32,2,320,128]{3,2,1,0:T(8,128)(2,1)} broadcast(bf16[32,320,128]{2,1,0:T(8,128)(2,1)} %bitcast_select_fusion), dimensions={0,2,3} | broadcast | bytes 7864320 | tf_op jit(solution)/shard_map/broadcast_in_dim | solution.py:282
  168.2 17.8 %all-to-all-start = ((bf16[128,160,128]{2,1,0:T(8,128)(2,1)}), bf16[128,160,128]{2,1,0:T(8,128)(2,1)}, u32[]{:S(2)}, u32[]{:S(2)}) async-start(bf16[128,160,128]{2,1,0:T(8,128)(2,1)} %bitcast.109), calls=%async_computation.1 | async-start | bytes 10485760 | tf_op jit(solution)/shard_map/all_to_all | solution.py:284
  191.1 4.9 %copy.106 = bf16[2,3,2048,256]{3,2,1,0:T(8,128)(2,1)S(1)} copy(bf16[2,3,2048,256]{3,1,0,2:T(4,128)(2,1)} %all-to-all-done.2) | data formatting | bytes 12582912 | tf_op jit(solution)/shard_map/all_to_all | solution.py:313
  199.3 5.2 %gather_fusion.1 = bf16[32,3,64,256]{3,2,1,0:T(8,128)(2,1)} fusion(bf16[64,3,64,256]{3,2,1,0:T(8,128)(2,1)} %bitcast.110, s32[1024]{0:T(1024)S(1)} %pad_clamp_fusion), kind=kCustom, calls=%fused_computation.3 | custom fusion | bytes 6291584 | tf_op jit(solution)/shard_map/jit(_take)/gather | solution.py:316
  204.5 3.9 broadcast_select_fusion
  208.4 41.5 %all-to-all-done = bf16[128,160,128]{2,1,0:T(8,128)(2,1)} async-done(((bf16[128,160,128]{2,1,0:T(8,128)(2,1)}), bf16[128,160,128]{2,1,0:T(8,128)(2,1)}, u32[]{:S(2)}, u32[]{:S(2)}) %all-to-all-start) | async-done | bytes 5242912 | tf_op jit(solution)/shard_map/all_to_all | solution.py:284
  249.9 5.0 %all-to-all-start.3 = ((bf16[32,3,64,256]{3,2,1,0:T(8,128)(2,1)}), bf16[32,3,64,256]{3,2,1,0:T(8,128)(2,1)}, u32[]{:S(2)}, u32[]{:S(2)}) async-start(bf16[32,3,64,256]{3,2,1,0:T(8,128)(2,1)} %broadcast_select_fusion), calls=%async_computation.4 | async-start | bytes 6291456 | tf_op jit(solution)/shard_map/all_to_all | solution.py:317
  255.0 8.8 %reshape.287 = bf16[1280,2048]{1,0:T(8,128)(2,1)} reshape(bf16[128,160,128]{2,1,0:T(8,128)(2,1)} %all-to-all-done) | data formatting | bytes 10485760 | tf_op jit(solution)/shard_map/reshape | solution.py:273
  263.8 5.6 %fusion.7 = f32[1280,256]{1,0:T(8,128)} fusion(bf16[1280,2048]{1,0:T(8,128)(2,1)} %reshape.287, bf16[2,3,2048,256]{3,2,1,0:T(8,128)(2,1)} %param.35, s32[]{:T(128)S(6)} %select_n.153), kind=kOutput, calls=%fused_computation.32 | convolution fusion | flops 1342177280 | bytes 7602180 | tf_op jit(solution)/shard_map/dot_general | solution.py:288
  272.2 11.2 %convolution_convert_fusion.1 = bf16[1280,2048]{1,0:T(8,128)(2,1)} fusion(bf16[1280,2048]{1,0:T(8,128)(2,1)} %reshape.287, f32[1280,256]{1,0:T(8,128)} %fusion.7, bf16[2,3,2048,256]{3,2,1,0:T(8,128)(2,1)} %param.35, s32[]{:T(128)S(6)} %select_n.153, s32[]{:T(128)S(6)} %add.206, s32[]{:T(128)S(6)} %add.205), kind=kOutput, calls=%fused_computation.9 | convolution fusion | flops 2688942080 | bytes 13895680 | tf_op jit(solution)/shard_map/dot_general | solution.py:291
  283.4 12.5 %add_convert_fusion = bf16[1280,2048]{1,0:T(8,128)(2,1)} fusion(bf16[1280,2048]{1,0:T(8,128)(2,1)} %convolution_convert_fusion.1, bf16[3,2048,256]{2,1,0:T(8,128)(2,1)} %collective-permute-done, f32[1280,256]{1,0:T(8,128)S(1)} %fusion.6, bf16[1280,2048]{1,0:T(8,128)(2,1)} %reshape.287), kind=kOutput, calls=%fused_computation.7 | convolution fusion | flops 2699427840 | bytes 19136512 | tf_op jit(solution)/shard_map/dot_general | solution.py:291
  295.9 8.9 %reshape.288 = bf16[128,160,128]{2,1,0:T(8,128)(2,1)} reshape(bf16[1280,2048]{1,0:T(8,128)(2,1)} %add_convert_fusion) | data formatting | bytes 10485760 | tf_op jit(solution)/shard_map/reshape | solution.py:270
  304.8 8.5 %all-to-all-start.1 = ((bf16[128,160,128]{2,1,0:T(8,128)(2,1)}), bf16[128,160,128]{2,1,0:T(8,128)(2,1)}, u32[]{:S(2)}, u32[]{:S(2)}) async-start(bf16[128,160,128]{2,1,0:T(8,128)(2,1)} %reshape.288), calls=%async_computation.2 | async-start | bytes 10485760 | tf_op jit(solution)/shard_map/all_to_all | solution.py:296
  313.5 4.0 copy.108
  317.4 59.8 %all-to-all-done.1 = bf16[128,160,128]{2,1,0:T(8,128)(2,1)} async-done(((bf16[128,160,128]{2,1,0:T(8,128)(2,1)}), bf16[128,160,128]{2,1,0:T(8,128)(2,1)}, u32[]{:S(2)}, u32[]{:S(2)}) %all-to-all-start.1) | async-done | bytes 5242912 | tf_op jit(solution)/shard_map/all_to_all | solution.py:296
  377.3 4.9 %gather_fusion.2 = bf16[512,16,128]{2,1,0:T(8,128)(2,1)} fusion(bf16[1280,16,128]{2,1,0:T(8,128)(2,1)} %bitcast.31, s32[1024]{0:T(1024)S(1)} %get-tuple-element.43), kind=kCustom, calls=%fused_computation.clone | custom fusion | bytes 4196352 | tf_op jit(solution)/shard_map/jit(_take)/gather | solution.py:304
  382.2 4.9 %gather_fusion.3 = bf16[512,16,128]{2,1,0:T(8,128)(2,1)} fusion(bf16[1280,16,128]{2,1,0:T(8,128)(2,1)} %bitcast.31, s32[1024]{0:T(1024)S(1)} %get-tuple-element.42), kind=kCustom, calls=%fused_computation.1.clone | custom fusion | bytes 4196352 | tf_op jit(solution)/shard_map/jit(_take)/gather | solution.py:304
  387.1 6.0 %multiply_reduce_fusion = f32[64,16,128]{2,1,0:T(8,128)S(1)} fusion(f32[64,8]{1,0:T(8,128)S(1)} %copy.104, bf16[512,16,128]{2,1,0:T(8,128)(2,1)} %gather_fusion.3, pred[512]{0:T(512)(128)(4,1)S(1)} %get-tuple-element.32, bf16[512,16,128]{2,1,0:T(8,128)(2,1)} %gather_fusion.2, pred[512]{0:T(512)(128)(4,1)S(1)} %get-tuple-element.16), kind=kLoop, calls=%fused_computation.10 | loop fusion | flops 7208960 | bytes 4721664 | tf_op jit(solution)/shard_map/reduce_sum | solution.py:306
  (122 shorter events, 44.2 us)
Async XLA Ops:
  7.2 52.7 %copy-start = (bf16[512,2048]{1,0:T(8,128)(2,1)S(1)}, bf16[512,2048]{1,0:T(8,128)(2,1)}, u32[]{:S(2)}) copy-start(bf16[512,2048]{1,0:T(8,128)(2,1)} %param.29) | copy-start | bytes 6291460
  42.4 6.2 %copy-start.14 = (s32[1,4]{1,0:T(1,128)S(1)}, s32[1,4]{1,0:T(1,128)}, u32[]{:S(2)}) copy-start(s32[1,4]{1,0:T(1,128)} %param.28) | copy-start | bytes 52
  42.4 6.9 %copy-start.6 = (bf16[256,512]{1,0:T(8,128)(2,1)S(1)}, bf16[256,512]{1,0:T(8,128)(2,1)}, u32[]{:S(2)}) copy-start(bf16[256,512]{1,0:T(8,128)(2,1)} %param.20) | copy-start | bytes 786436
  42.4 7.2 %copy-start.7 = (bf16[256,512]{1,0:T(8,128)(2,1)S(1)}, bf16[256,512]{1,0:T(8,128)(2,1)}, u32[]{:S(2)}) copy-start(bf16[256,512]{1,0:T(8,128)(2,1)} %param.21) | copy-start | bytes 786436
  42.4 120.2 %all-to-all-start.2 = ((bf16[2,3,2048,256]{3,1,0,2:T(4,128)(2,1)}), bf16[2,3,2048,256]{3,1,0,2:T(4,128)(2,1)}, u32[]{:S(2)}, u32[]{:S(2)}) async-start(bf16[2,3,2048,256]{3,1,0,2:T(4,128)(2,1)} %copy.105), calls=%async_computation.3 | async-start | bytes 16777216 | tf_op jit(solution)/shard_map/all_to_all | solution.py:313
  47.5 2.5 copy-start.5
  47.5 67.9 %reduce-scatter.2.cloned.1.call-start = ((), (), s32[]{:S(2)}) async-start(), calls=%async_computation.5 | async-start | bytes 2621440 | tf_op jit(solution)/shard_map/reduce_scatter | solution.py:233
  48.8 0.5 copy-start.13
  53.1 2.0 copy-start.8
  55.5 2.8 copy-start.9
  59.9 2.1 copy-start.11
  59.9 3.9 copy-start.15
  59.9 55.5 %copy-start.4 = (bf16[64,2048]{1,0:T(8,128)(2,1)S(1)}, bf16[64,2048]{1,0:T(8,128)(2,1)}, u32[]{:S(2)}) copy-start(bf16[64,2048]{1,0:T(8,128)(2,1)} %param.19) | copy-start | bytes 786436
  59.9 56.8 %copy-start.10 = (f32[2048]{0:T(1024)S(1)}, f32[2048]{0:T(1024)}, u32[]{:S(2)}) copy-start(f32[2048]{0:T(1024)} %param.30) | copy-start | bytes 24580
  168.2 81.8 %all-to-all-start = ((bf16[128,160,128]{2,1,0:T(8,128)(2,1)}), bf16[128,160,128]{2,1,0:T(8,128)(2,1)}, u32[]{:S(2)}, u32[]{:S(2)}) async-start(bf16[128,160,128]{2,1,0:T(8,128)(2,1)} %bitcast.109), calls=%async_computation.1 | async-start | bytes 10485760 | tf_op jit(solution)/shard_map/all_to_all | solution.py:284
  186.0 4.9 %copy-start.16 = (s32[32]{0:T(128)S(1)}, s32[32]{0:T(128)}, u32[]{:S(2)}) copy-start(s32[32]{0:T(128)} %param.34) | copy-start | bytes 388
  189.8 79.6 %collective-permute-start = (bf16[3,2048,256]{2,1,0:T(8,128)(2,1)}, bf16[3,2048,256]{2,1,0:T(8,128)(2,1)}, u32[]{:S(2)}, u32[]{:S(2)}) collective-permute-start(bf16[3,2048,256]{2,1,0:T(8,128)(2,1)} %dynamic-slice_bitcast_fusion), channel_id=1, source_target_pairs={{0,1},{1,0},{2,3},{3,2},{4,5},{5,4},{6,7},{7,6},{8,9},{9,8},{10,11... | collective-permute-start | bytes 9437192 | tf_op jit(solution)/shard_map/ppermute | solution.py:265
  249.9 54.9 %all-to-all-start.3 = ((bf16[32,3,64,256]{3,2,1,0:T(8,128)(2,1)}), bf16[32,3,64,256]{3,2,1,0:T(8,128)(2,1)}, u32[]{:S(2)}, u32[]{:S(2)}) async-start(bf16[32,3,64,256]{3,2,1,0:T(8,128)(2,1)} %broadcast_select_fusion), calls=%async_computation.4 | async-start | bytes 6291456 | tf_op jit(solution)/shard_map/all_to_all | solution.py:317
  263.8 5.6 %copy-start.2 = (bf16[1280,2048]{1,0:T(8,128)(2,1)S(1)}, bf16[1280,2048]{1,0:T(8,128)(2,1)}, u32[]{:S(2)}) copy-start(bf16[1280,2048]{1,0:T(8,128)(2,1)} %reshape.287) | copy-start | bytes 15728644
  304.8 8.5 %copy-start.12 = (f32[64,8]{0,1:T(8,128)S(1)}, f32[64,8]{0,1:T(8,128)}, u32[]{:S(2)}) copy-start(f32[64,8]{0,1:T(8,128)} %param.32) | copy-start | bytes 6148
  304.8 72.5 %all-to-all-start.1 = ((bf16[128,160,128]{2,1,0:T(8,128)(2,1)}), bf16[128,160,128]{2,1,0:T(8,128)(2,1)}, u32[]{:S(2)}, u32[]{:S(2)}) async-start(bf16[128,160,128]{2,1,0:T(8,128)(2,1)} %reshape.288), calls=%async_computation.2 | async-start | bytes 10485760 | tf_op jit(solution)/shard_map/all_to_all | solution.py:296
  387.1 6.0 %copy-start.3 = (f32[64,2048]{1,0:T(8,128)S(1)}, f32[64,2048]{1,0:T(8,128)}, u32[]{:S(2)}) copy-start(f32[64,2048]{1,0:T(8,128)} %reduce-scatter.2.cloned.1.call-done) | copy-start | bytes 1572868
  387.1 6.9 %copy-start.1 = (bf16[512,2048]{1,0:T(8,128)(2,1)S(1)}, bf16[512,2048]{1,0:T(8,128)(2,1)}, u32[]{:S(2)}) copy-start(bf16[512,2048]{1,0:T(8,128)(2,1)} %param.29) | copy-start | bytes 6291460
Sparse Core Ops, SparseCore 0:
  62.2 53.2 reduce-scatter.1
where the time goes:
time: 403 us; the launch traced here: 401 us
  waiting for transfers between devices  183 us (45%)
  local copies, waits for them, and re-layouts  80.1 us (20%)
  matrix products  38.5 us (10%)
  starting transfers between devices  37.6 us (9%)
  other arithmetic  26.6 us (7%)
  Pallas kernels  20.2 us (5%)
  between operations  14.6 us (4%)
    all_to_all x1, waiting for transfers between devices, body(): lax.all_to_all(partial_value, ('req', 'exp'), split_axis=0, concat_axis=0...  59.8 us
    reduce_scatter x1, waiting for transfers between devices, body(): lax.psum_scatter(jnp.dot(attended, out_proj, preferred_element_type=jnp.f...  45.9 us
    all_to_all x1, waiting for transfers between devices, body(): lax.all_to_all(copies, ('req', 'exp'), split_axis=0, concat_axis=0, tiled...  41.5 us
    all_to_all x1, waiting for transfers between devices, body(): lax.all_to_all(slot_weights, 'req', split_axis=2, concat_axis=0, tiled=True)  36 us
    dot_general x2, matrix products, body(): lax.dot_general(hidden, part[2], (((1,), (1,)), ((), ())), preferred_elem...  23.7 us
    pallas_call x1, Pallas kernels, exchange_cache(): pl.pallas_call(functools.partial(cache_kernel, n), out_shape=jax.ShapeDty...  20.2 us
    all_to_all x1, starting transfers between devices, body(): lax.all_to_all(copies, ('req', 'exp'), split_axis=0, concat_axis=0, tiled...  17.8 us
    optimization_barrier x1, local copies, waits for them, and re-layouts, body(): slot_weights, gathered = lax.optimization_barrier((slot_weights, gathered))  10.5 us
  transfers between devices with their start and end apart: 6, of which 4 were waited for; matrix products, arithmetic and copies ran while one was open for 27% of the time, Pallas kernels for 0%

commit v1 on v0

--- a/solution.py
+++ b/solution.py
@@ -310,11 +310,26 @@
     )
     residual_tiles = residual.reshape(tok_dev, tile_high, lanes)
     layer_out = (residual_tiles + mixture).astype(jnp.bfloat16).reshape(tok_dev, model_width)
-    spread_slots = lax.all_to_all(slot_weights, "req", split_axis=2, concat_axis=0, tiled=True)
+    stacked_rows = slot_weights.shape[1] * slot_weights.shape[2]
+    piece_rows = stacked_rows // req_count
+    spread = [
+        lax.all_to_all(
+            slot_weights[c].reshape(req_count, piece_rows, slot_weights.shape[3]),
+            "req",
+            split_axis=0,
+            concat_axis=0,
+            tiled=True,
+        )
+        for c in range(slots_here)
+    ]
+    spread_slots = jnp.stack(spread, axis=1).reshape(
+        slot_total, piece_rows, slot_weights.shape[3]
+    )
     replica_onehot = new_replicas[:, None] == slot_range[None, :]
     source_slot = jnp.sum(jnp.where(replica_onehot, slot_of[None, :], 0), axis=1)
     chosen_pieces = jnp.take(spread_slots, source_slot, axis=0)
-    replica_weights = lax.all_to_all(chosen_pieces, "req", split_axis=0, concat_axis=2, tiled=True)
+    replica_weights = lax.all_to_all(chosen_pieces, "req", split_axis=0, concat_axis=0, tiled=True)
+    replica_weights = replica_weights.reshape((1,) + slot_weights.shape[1:])
     return (layer_out, replica_weights)
 
 

time: 403 us -> 367 us (0.911)
  local copies, waits for them, and re-layouts: 80.1 us -> 62.6 us
  waiting for transfers between devices: 183 us -> 166 us
  other arithmetic: 26.6 us -> 32.2 us
  starting transfers between devices: 37.6 us -> 32.2 us
    reduce_scatter x1, waiting for transfers between devices: 45.9 us -> 11 us  [body(): lax.psum_scatter(jnp.dot(attended, out_proj, preferred_element_type=jnp.f...]
    all_to_all x3 -> x0, local copies, waits for them, and re-layouts: 12.2 us -> none  [the longest x2 8.18 us: body(): lax.all_to_all(slot_weights, 'req', split_axis=2, concat_axis=0, tiled=True)]
    optimization_barrier x1 -> x0, local copies, waits for them, and re-layouts: 10.5 us -> none  [body(): slot_weights, gathered = lax.optimization_barrier((slot_weights, gathered))]
    all_to_all x1, starting transfers between devices: 17.8 us -> 7.36 us  [body(): lax.all_to_all(copies, ('req', 'exp'), split_axis=0, concat_axis=0, tiled...]
    all_to_all x2 -> x3, waiting for transfers between devices: 36 us -> 43.5 us  [the longest x2 43.5 us: body(): lax.all_to_all(slot_weights[c].reshape(req_count, piece_rows, slot_weight...]
    slice x1 -> x2, local copies, waits for them, and re-layouts: 0.23 us -> 6.7 us  [the longest x1 6.47 us: body(): slot_weights[c].reshape(req_count, piece_rows, slot_weights.shape[3])]
    another operation x4 -> x5, other arithmetic: 2.56 us -> 8.66 us  [the longest x1 6.09 us: body(): jnp.stack(spread, axis=1)]
    all_to_all x1, waiting for transfers between devices: 41.5 us -> 47.3 us  [body(): lax.all_to_all(copies, ('req', 'exp'), split_axis=0, concat_axis=0, tiled...]
  transfers between devices with their start and end apart: 6 -> 7, of which waited for: 4 -> 5; matrix products, arithmetic and copies ran while one was open for 27% -> 27% of each run, Pallas kernels for 0% -> 0%
where the time goes in v1:
time: 367 us; the launch traced here: 366 us
  waiting for transfers between devices  166 us (45%)
  local copies, waits for them, and re-layouts  62.6 us (17%)
  matrix products  38.5 us (10%)
  other arithmetic  32.2 us (9%)
  starting transfers between devices  32.2 us (9%)
  Pallas kernels  20.2 us (6%)
  between operations  14.6 us (4%)
    all_to_all x1, waiting for transfers between devices, body(): lax.all_to_all(partial_value, ('req', 'exp'), split_axis=0, concat_axis=0...  63.8 us
    all_to_all x1, waiting for transfers between devices, body(): lax.all_to_all(copies, ('req', 'exp'), split_axis=0, concat_axis=0, tiled...  47.3 us
    all_to_all x2, waiting for transfers between devices, body(): lax.all_to_all(slot_weights[c].reshape(req_count, piece_rows, slot_weight...  43.5 us
    dot_general x2, matrix products, body(): lax.dot_general(hidden, part[2], (((1,), (1,)), ((), ())), preferred_elem...  23.6 us
    pallas_call x1, Pallas kernels, exchange_cache(): pl.pallas_call(functools.partial(cache_kernel, n), out_shape=jax.ShapeDty...  20.2 us
    reduce_scatter x1, waiting for transfers between devices, body(): lax.psum_scatter(jnp.dot(attended, out_proj, preferred_element_type=jnp.f...  11 us
    all_to_all x2, starting transfers between devices, body(): lax.all_to_all(slot_weights[c].reshape(req_count, piece_rows, slot_weight...  10.1 us
    reshape x1, local copies, waits for them, and re-layouts, as_tiles(): return rows.reshape(req_count * exp_count, tile_rows, lanes)  8.93 us
  transfers between devices with their start and end apart: 7, of which 5 were waited for; matrix products, arithmetic and copies ran while one was open for 27% of the time, Pallas kernels for 0%

profile of v1, /device:TPU:1, one launch (start us, length us, event | category | flops | bytes accessed | tf_op | source)
XLA Modules:
  0.0 365.8 jit_solution(3979987059142014665)
XLA Ops:
  11.8 20.2 %shard_map.176 = bf16[32,2,1024]{2,1,0:T(2,128)(2,1)} custom-call(s32[64]{0:T(128)} %reshape.283.need_ref, bf16[32,2,1024]{2,1,0:T(2,128)(2,1)} %maximum_bitcast_fusion.both_ref), custom_call_target="tpu_custom_call" | custom-call | tf_op jit(solution)/shard_map/pallas_call | solution.py:107
  32.0 6.5 %fusion.63 = (bf16[1,3,2048,256]{3,2,1,0:T(8,128)(2,1)}, bf16[1,3,2048,256]{3,2,1,0:T(8,128)(2,1)}, bf16[3,2048,256]{2,1,0:T(8,128)(2,1)}) fusion(bf16[2,3,2048,256]{3,2,1,0:T(8,128)(2,1)} %param.35, s32[]{:T(128)S(6)} %select_n.154), kind=kLoop, calls=%fused_computation.154 | loop fusion | bytes 18874372 | tf_op jit(solution)/shard_map/slice | solution.py:317
  38.4 5.0 %all-to-all-start.2 = ((bf16[32,192,256]{2,1,0:T(8,128)(2,1)}), bf16[32,192,256]{2,1,0:T(8,128)(2,1)}, u32[]{:S(2)}, u32[]{:S(2)}) async-start(bf16[32,192,256]{2,1,0:T(8,128)(2,1)} %bitcast.109), calls=%async_computation.3 | async-start | bytes 6291456 | tf_op jit(solution)/shard_map/all_to_all | solution.py:316
  57.8 24.2 %all-to-all-done.2 = bf16[32,192,256]{2,1,0:T(8,128)(2,1)} async-done(((bf16[32,192,256]{2,1,0:T(8,128)(2,1)}), bf16[32,192,256]{2,1,0:T(8,128)(2,1)}, u32[]{:S(2)}, u32[]{:S(2)}) %all-to-all-start.2) | async-done | bytes 3145760 | tf_op jit(solution)/shard_map/all_to_all | solution.py:316
  82.0 5.1 %all-to-all-start.3 = ((bf16[32,192,256]{2,1,0:T(8,128)(2,1)}), bf16[32,192,256]{2,1,0:T(8,128)(2,1)}, u32[]{:S(2)}, u32[]{:S(2)}) async-start(bf16[32,192,256]{2,1,0:T(8,128)(2,1)} %bitcast.108), calls=%async_computation.4 | async-start | bytes 6291456 | tf_op jit(solution)/shard_map/all_to_all | solution.py:316
  94.7 11.0 %reduce-scatter.2.cloned.1.call-done = f32[64,2048]{1,0:T(8,128)} async-done(((f32[256,2048]{1,0:T(8,128)}), f32[64,2048]{1,0:T(8,128)}) %reduce-scatter.2.cloned.1.call-update) | async-done | bytes 524304 | tf_op jit(solution)/shard_map/reduce_scatter | solution.py:233
  111.4 5.4 %bitcast_select_fusion = bf16[32,320,128]{2,1,0:T(8,128)(2,1)} fusion(pred[32,320]{1,0:T(8,128)(4,1)S(1)} %copy.59, bf16[32,320,128]{2,1,0:T(8,128)(2,1)} %bitcast.110), kind=kLoop, calls=%fused_computation.16 | loop fusion | flops 1310720 | bytes 5253120 | tf_op jit(solution)/shard_map/jit(_where)/select_n | solution.py:280
  116.8 19.3 %all-to-all-done.3 = bf16[32,192,256]{2,1,0:T(8,128)(2,1)} async-done(((bf16[32,192,256]{2,1,0:T(8,128)(2,1)}), bf16[32,192,256]{2,1,0:T(8,128)(2,1)}, u32[]{:S(2)}, u32[]{:S(2)}) %all-to-all-start.3) | async-done | bytes 3145760 | tf_op jit(solution)/shard_map/all_to_all | solution.py:316
  136.1 5.5 %broadcast_in_dim.211 = bf16[32,2,320,128]{3,2,1,0:T(8,128)(2,1)} broadcast(bf16[32,320,128]{2,1,0:T(8,128)(2,1)} %bitcast_select_fusion), dimensions={0,2,3} | broadcast | bytes 7864320 | tf_op jit(solution)/shard_map/broadcast_in_dim | solution.py:282
  141.7 7.4 %all-to-all-start = ((bf16[128,160,128]{2,1,0:T(8,128)(2,1)}), bf16[128,160,128]{2,1,0:T(8,128)(2,1)}, u32[]{:S(2)}, u32[]{:S(2)}) async-start(bf16[128,160,128]{2,1,0:T(8,128)(2,1)} %bitcast.106), calls=%async_computation.1 | async-start | bytes 10485760 | tf_op jit(solution)/shard_map/all_to_all | solution.py:284
  150.4 6.1 %pad_maximum_fusion = bf16[32,2,192,256]{3,2,1,0:T(8,128)(2,1)} fusion(bf16[32,1,192,256]{3,2,1,0:T(8,128)(2,1)} %bitcast.36, bf16[32,1,192,256]{3,2,1,0:T(8,128)(2,1)} %bitcast.34), kind=kLoop, calls=%fused_computation.10 | loop fusion | flops 3145728 | bytes 12582912 | tf_op jit(solution)/shard_map/stack | solution.py:325
  156.5 5.2 %gather_fusion.1 = bf16[32,192,256]{2,1,0:T(8,128)(2,1)} fusion(bf16[64,192,256]{2,1,0:T(8,128)(2,1)} %bitcast.107, s32[1024]{0:T(1024)S(1)} %pad_clamp_fusion), kind=kCustom, calls=%fused_computation.3 | custom fusion | bytes 6291584 | tf_op jit(solution)/shard_map/jit(_take)/gather | solution.py:330
  161.7 3.9 %broadcast_select_fusion = bf16[32,192,256]{2,1,0:T(8,128)(2,1)} fusion(bf16[32,192,256]{2,1,0:T(8,128)(2,1)} %gather_fusion.1, pred[32]{0:T(512)(128)(4,1)S(1)} %compare_and_fusion.4), kind=kLoop, calls=%fused_computation.14 | loop fusion | flops 1572864 | bytes 6291488 | tf_op jit(solution)/shard_map/jit(_take)/select_n | solution.py:330
  165.7 47.3 %all-to-all-done = bf16[128,160,128]{2,1,0:T(8,128)(2,1)} async-done(((bf16[128,160,128]{2,1,0:T(8,128)(2,1)}), bf16[128,160,128]{2,1,0:T(8,128)(2,1)}, u32[]{:S(2)}, u32[]{:S(2)}) %all-to-all-start) | async-done | bytes 5242912 | tf_op jit(solution)/shard_map/all_to_all | solution.py:284
  213.0 4.8 %all-to-all-start.4 = ((bf16[32,192,256]{2,1,0:T(8,128)(2,1)}), bf16[32,192,256]{2,1,0:T(8,128)(2,1)}, u32[]{:S(2)}, u32[]{:S(2)}) async-start(bf16[32,192,256]{2,1,0:T(8,128)(2,1)} %broadcast_select_fusion), calls=%async_computation.5 | async-start | bytes 6291456 | tf_op jit(solution)/shard_map/all_to_all | solution.py:331
  217.8 8.8 %reshape.293 = bf16[1280,2048]{1,0:T(8,128)(2,1)} reshape(bf16[128,160,128]{2,1,0:T(8,128)(2,1)} %all-to-all-done) | data formatting | bytes 10485760 | tf_op jit(solution)/shard_map/reshape | solution.py:273
  226.6 5.5 %fusion.7 = f32[1280,256]{1,0:T(8,128)} fusion(bf16[1280,2048]{1,0:T(8,128)(2,1)} %reshape.293, bf16[2,3,2048,256]{3,2,1,0:T(8,128)(2,1)} %param.35, s32[]{:T(128)S(6)} %select_n.153), kind=kOutput, calls=%fused_computation.33 | convolution fusion | flops 1342177280 | bytes 7602180 | tf_op jit(solution)/shard_map/dot_general | solution.py:288
  235.0 11.2 %convolution_convert_fusion.1 = bf16[1280,2048]{1,0:T(8,128)(2,1)} fusion(bf16[1280,2048]{1,0:T(8,128)(2,1)} %reshape.293, f32[1280,256]{1,0:T(8,128)} %fusion.7, bf16[2,3,2048,256]{3,2,1,0:T(8,128)(2,1)} %param.35, s32[]{:T(128)S(6)} %select_n.153, s32[]{:T(128)S(6)} %add.206, s32[]{:T(128)S(6)} %add.205), kind=kOutput, calls=%fused_computation.9 | convolution fusion | flops 2688942080 | bytes 13895680 | tf_op jit(solution)/shard_map/dot_general | solution.py:291
  246.1 12.5 %add_convert_fusion = bf16[1280,2048]{1,0:T(8,128)(2,1)} fusion(bf16[1280,2048]{1,0:T(8,128)(2,1)} %convolution_convert_fusion.1, bf16[3,2048,256]{2,1,0:T(8,128)(2,1)} %collective-permute-done, f32[1280,256]{1,0:T(8,128)S(1)} %fusion.6, bf16[1280,2048]{1,0:T(8,128)(2,1)} %reshape.293), kind=kOutput, calls=%fused_computation.7 | convolution fusion | flops 2699427840 | bytes 19136512 | tf_op jit(solution)/shard_map/dot_general | solution.py:291
  258.6 8.9 %reshape.294 = bf16[128,160,128]{2,1,0:T(8,128)(2,1)} reshape(bf16[1280,2048]{1,0:T(8,128)(2,1)} %add_convert_fusion) | data formatting | bytes 10485760 | tf_op jit(solution)/shard_map/reshape | solution.py:270
  267.5 8.7 %all-to-all-start.1 = ((bf16[128,160,128]{2,1,0:T(8,128)(2,1)}), bf16[128,160,128]{2,1,0:T(8,128)(2,1)}, u32[]{:S(2)}, u32[]{:S(2)}) async-start(bf16[128,160,128]{2,1,0:T(8,128)(2,1)} %reshape.294), calls=%async_computation.2 | async-start | bytes 10485760 | tf_op jit(solution)/shard_map/all_to_all | solution.py:296
  276.4 63.8 %all-to-all-done.1 = bf16[128,160,128]{2,1,0:T(8,128)(2,1)} async-done(((bf16[128,160,128]{2,1,0:T(8,128)(2,1)}), bf16[128,160,128]{2,1,0:T(8,128)(2,1)}, u32[]{:S(2)}, u32[]{:S(2)}) %all-to-all-start.1) | async-done | bytes 5242912 | tf_op jit(solution)/shard_map/all_to_all | solution.py:296
  343.9 4.9 %gather_fusion.3 = bf16[512,16,128]{2,1,0:T(8,128)(2,1)} fusion(bf16[1280,16,128]{2,1,0:T(8,128)(2,1)} %bitcast.31, s32[1024]{0:T(1024)S(1)} %get-tuple-element.45), kind=kCustom, calls=%fused_computation.1.clone | custom fusion | bytes 4196352 | tf_op jit(solution)/shard_map/jit(_take)/gather | solution.py:304
  348.7 5.6 %multiply_reduce_fusion = f32[64,16,128]{2,1,0:T(8,128)S(1)} fusion(f32[64,8]{1,0:T(8,128)S(1)} %copy.60, bf16[512,16,128]{2,1,0:T(8,128)(2,1)} %gather_fusion.3, pred[512]{0:T(512)(128)(4,1)S(1)} %get-tuple-element.35, bf16[512,16,128]{2,1,0:T(8,128)(2,1)S(1)} %gather_fusion.2, pred[512]{0:T(512)(128)(4,1)S(1)} %get-tuple-element.16), kind=kLoop, calls=%fused_computation.11 | loop fusion | flops 7208960 | bytes 4721664 | tf_op jit(solution)/shard_map/reduce_sum | solution.py:306
  (122 shorter events, 44.6 us)
Async XLA Ops:
  7.2 48.5 %copy-start = (bf16[512,2048]{1,0:T(8,128)(2,1)S(1)}, bf16[512,2048]{1,0:T(8,128)(2,1)}, u32[]{:S(2)}) copy-start(bf16[512,2048]{1,0:T(8,128)(2,1)} %param.29) | copy-start | bytes 6291460
  38.4 5.9 %copy-start.14 = (s32[1,4]{1,0:T(1,128)S(1)}, s32[1,4]{1,0:T(1,128)}, u32[]{:S(2)}) copy-start(s32[1,4]{1,0:T(1,128)} %param.28) | copy-start | bytes 52
  38.4 6.7 %copy-start.6 = (bf16[256,512]{1,0:T(8,128)(2,1)S(1)}, bf16[256,512]{1,0:T(8,128)(2,1)}, u32[]{:S(2)}) copy-start(bf16[256,512]{1,0:T(8,128)(2,1)} %param.20) | copy-start | bytes 786436
  38.4 7.0 %copy-start.7 = (bf16[256,512]{1,0:T(8,128)(2,1)S(1)}, bf16[256,512]{1,0:T(8,128)(2,1)}, u32[]{:S(2)}) copy-start(bf16[256,512]{1,0:T(8,128)(2,1)} %param.21) | copy-start | bytes 786436
  38.4 43.5 %all-to-all-start.2 = ((bf16[32,192,256]{2,1,0:T(8,128)(2,1)}), bf16[32,192,256]{2,1,0:T(8,128)(2,1)}, u32[]{:S(2)}, u32[]{:S(2)}) async-start(bf16[32,192,256]{2,1,0:T(8,128)(2,1)} %bitcast.109), calls=%async_computation.3 | async-start | bytes 6291456 | tf_op jit(solution)/shard_map/all_to_all | solution.py:316
  43.4 2.4 copy-start.5
  43.4 62.2 %reduce-scatter.2.cloned.1.call-start = ((), (), s32[]{:S(2)}) async-start(), calls=%async_computation.6 | async-start | bytes 2621440 | tf_op jit(solution)/shard_map/reduce_scatter | solution.py:233
  44.5 0.5 copy-start.13
  48.9 2.0 copy-start.8
  51.2 2.8 copy-start.9
  82.0 5.2 %copy-start.11 = (s32[64,8]{0,1:T(8,128)S(1)}, s32[64,8]{0,1:T(8,128)}, u32[]{:S(2)}) copy-start(s32[64,8]{0,1:T(8,128)} %param.31) | copy-start | bytes 6148
  82.0 6.9 %copy-start.15 = (s32[64]{0:T(128)S(1)}, s32[64]{0:T(128)}, u32[]{:S(2)}) copy-start(s32[64]{0:T(128)} %param.33) | copy-start | bytes 772
  82.0 23.6 %copy-start.4 = (bf16[64,2048]{1,0:T(8,128)(2,1)S(1)}, bf16[64,2048]{1,0:T(8,128)(2,1)}, u32[]{:S(2)}) copy-start(bf16[64,2048]{1,0:T(8,128)(2,1)} %param.19) | copy-start | bytes 786436
  82.0 24.9 %copy-start.10 = (f32[2048]{0:T(1024)S(1)}, f32[2048]{0:T(1024)}, u32[]{:S(2)}) copy-start(f32[2048]{0:T(1024)} %param.30) | copy-start | bytes 24580
  82.0 54.1 %all-to-all-start.3 = ((bf16[32,192,256]{2,1,0:T(8,128)(2,1)}), bf16[32,192,256]{2,1,0:T(8,128)(2,1)}, u32[]{:S(2)}, u32[]{:S(2)}) async-start(bf16[32,192,256]{2,1,0:T(8,128)(2,1)} %bitcast.108), calls=%async_computation.4 | async-start | bytes 6291456 | tf_op jit(solution)/shard_map/all_to_all | solution.py:316
  141.7 8.6 %copy-start.16 = (s32[32]{0:T(128)S(1)}, s32[32]{0:T(128)}, u32[]{:S(2)}) copy-start(s32[32]{0:T(128)} %param.34) | copy-start | bytes 388
  141.7 71.3 %all-to-all-start = ((bf16[128,160,128]{2,1,0:T(8,128)(2,1)}), bf16[128,160,128]{2,1,0:T(8,128)(2,1)}, u32[]{:S(2)}, u32[]{:S(2)}) async-start(bf16[128,160,128]{2,1,0:T(8,128)(2,1)} %bitcast.106), calls=%async_computation.1 | async-start | bytes 10485760 | tf_op jit(solution)/shard_map/all_to_all | solution.py:284
  149.0 83.1 %collective-permute-start = (bf16[3,2048,256]{2,1,0:T(8,128)(2,1)}, bf16[3,2048,256]{2,1,0:T(8,128)(2,1)}, u32[]{:S(2)}, u32[]{:S(2)}) collective-permute-start(bf16[3,2048,256]{2,1,0:T(8,128)(2,1)} %get-tuple-element.24), channel_id=1, source_target_pairs={{0,1},{1,0},{2,3},{3,2},{4,5},{5,4},{6,7},{7,6},{8,9},{9,8},{10,11... | collective-permute-start | bytes 9437192 | tf_op jit(solution)/shard_map/ppermute | solution.py:265
  213.0 54.6 %all-to-all-start.4 = ((bf16[32,192,256]{2,1,0:T(8,128)(2,1)}), bf16[32,192,256]{2,1,0:T(8,128)(2,1)}, u32[]{:S(2)}, u32[]{:S(2)}) async-start(bf16[32,192,256]{2,1,0:T(8,128)(2,1)} %broadcast_select_fusion), calls=%async_computation.5 | async-start | bytes 6291456 | tf_op jit(solution)/shard_map/all_to_all | solution.py:331
  226.6 5.5 %copy-start.2 = (bf16[1280,2048]{1,0:T(8,128)(2,1)S(1)}, bf16[1280,2048]{1,0:T(8,128)(2,1)}, u32[]{:S(2)}) copy-start(bf16[1280,2048]{1,0:T(8,128)(2,1)} %reshape.293) | copy-start | bytes 15728644
  267.5 8.7 %copy-start.12 = (f32[64,8]{0,1:T(8,128)S(1)}, f32[64,8]{0,1:T(8,128)}, u32[]{:S(2)}) copy-start(f32[64,8]{0,1:T(8,128)} %param.32) | copy-start | bytes 6148
  267.5 72.7 %all-to-all-start.1 = ((bf16[128,160,128]{2,1,0:T(8,128)(2,1)}), bf16[128,160,128]{2,1,0:T(8,128)(2,1)}, u32[]{:S(2)}, u32[]{:S(2)}) async-start(bf16[128,160,128]{2,1,0:T(8,128)(2,1)} %reshape.294), calls=%async_computation.2 | async-start | bytes 10485760 | tf_op jit(solution)/shard_map/all_to_all | solution.py:296
  348.7 5.6 %copy-start.3 = (f32[64,2048]{1,0:T(8,128)S(1)}, f32[64,2048]{1,0:T(8,128)}, u32[]{:S(2)}) copy-start(f32[64,2048]{1,0:T(8,128)} %reduce-scatter.2.cloned.1.call-done) | copy-start | bytes 1572868
  354.3 4.7 %copy-start.1 = (bf16[512,2048]{1,0:T(8,128)(2,1)S(1)}, bf16[512,2048]{1,0:T(8,128)(2,1)}, u32[]{:S(2)}) copy-start(bf16[512,2048]{1,0:T(8,128)(2,1)} %param.29) | copy-start | bytes 6291460
Sparse Core Ops, SparseCore 0:
  57.9 47.7 reduce-scatter.1

commit v2 on v1

--- a/solution.py
+++ b/solution.py
@@ -277,9 +277,16 @@
     row_token = jnp.arange(tok_dev * topk_count, dtype=jnp.int32) // topk_count
     source_token = jnp.zeros((slot_total * capacity,), jnp.int32).at[target].set(row_token)
     filled = jnp.zeros((slot_total * capacity,), jnp.bool_).at[target].set(True)
-    outbox = jnp.where(filled[:, None, None], normed_tiles[source_token], jnp.bfloat16(0))
-    outbox = outbox.reshape(req_count, 1, slots_here * tile_rows, lanes)
-    copies = jnp.broadcast_to(outbox, (req_count, pair_count, slots_here * tile_rows, lanes))
+    per_req = slots_here * capacity
+    copy_token = jnp.broadcast_to(
+        source_token.reshape(req_count, 1, per_req), (req_count, pair_count, per_req)
+    )
+    copy_filled = jnp.broadcast_to(
+        filled.reshape(req_count, 1, per_req), (req_count, pair_count, per_req)
+    )
+    copies = jnp.where(
+        copy_filled[..., None, None], normed_tiles[copy_token], jnp.bfloat16(0)
+    )
     copies = copies.reshape(req_count * exp_count, tile_rows, lanes)
     inbox = lax.all_to_all(copies, ("req", "exp"), split_axis=0, concat_axis=0, tiled=True)
     in_rows = as_rows(inbox)

time: 367 us -> 363 us (0.989)
  waiting for transfers between devices: 166 us -> 158 us
  other arithmetic: 32.2 us -> 38 us
    all_to_all x2, waiting for transfers between devices: 43.5 us -> 31.4 us  [body(): lax.all_to_all(slot_weights[c].reshape(req_count, piece_rows, slot_weight...]
    broadcast_in_dim x5 -> x3, local copies, waits for them, and re-layouts: 5.88 us -> 0.65 us  [the longest x2 0.56 us: body(): jnp.where(copy_filled[..., None, None], normed_tiles[copy_token], jnp.bfl...]
    reduce_scatter x1, waiting for transfers between devices: 11 us -> 15.4 us  [body(): lax.psum_scatter(jnp.dot(attended, out_proj, preferred_element_type=jnp.f...]
    select_n x2, other arithmetic: 5.42 us -> 9.46 us  [the longest x1 9.43 us: body(): jnp.where(copy_filled[..., None, None], normed_tiles[copy_token], jnp.bfl...]
  transfers between devices with their start and end apart: 7 -> 7, of which waited for: 5 -> 5; matrix products, arithmetic and copies ran while one was open for 27% -> 30% of each run, Pallas kernels for 0% -> 0%
where the time goes in v2:
time: 363 us; the launch traced here: 361 us
  waiting for transfers between devices  158 us (44%)
  local copies, waits for them, and re-layouts  60.4 us (17%)
  other arithmetic  38 us (10%)
  matrix products  38 us (10%)
  starting transfers between devices  31.8 us (9%)
  Pallas kernels  20.2 us (6%)
  between operations  14.6 us (4%)
    all_to_all x1, waiting for transfers between devices, body(): lax.all_to_all(partial_value, ('req', 'exp'), split_axis=0, concat_axis=0...  63.8 us
    all_to_all x1, waiting for transfers between devices, body(): lax.all_to_all(copies, ('req', 'exp'), split_axis=0, concat_axis=0, tiled...  47.3 us
    all_to_all x2, waiting for transfers between devices, body(): lax.all_to_all(slot_weights[c].reshape(req_count, piece_rows, slot_weight...  31.4 us
    dot_general x2, matrix products, body(): lax.dot_general(hidden, part[2], (((1,), (1,)), ((), ())), preferred_elem...  23.6 us
    pallas_call x1, Pallas kernels, exchange_cache(): pl.pallas_call(functools.partial(cache_kernel, n), out_shape=jax.ShapeDty...  20.2 us
    reduce_scatter x1, waiting for transfers between devices, body(): lax.psum_scatter(jnp.dot(attended, out_proj, preferred_element_type=jnp.f...  15.4 us
    all_to_all x2, starting transfers between devices, body(): lax.all_to_all(slot_weights[c].reshape(req_count, piece_rows, slot_weight...  10.1 us
    select_n x1, other arithmetic, body(): jnp.where(copy_filled[..., None, None], normed_tiles[copy_token], jnp.bfl...  9.43 us
  transfers between devices with their start and end apart: 7, of which 5 were waited for; matrix products, arithmetic and copies ran while one was open for 30% of the time, Pallas kernels for 0%

profile of v2, /device:TPU:1, one launch (start us, length us, event | category | flops | bytes accessed | tf_op | source)
XLA Modules:
  0.0 360.8 jit_solution(16580847970306642764)
XLA Ops:
  11.8 20.2 %shard_map.176 = bf16[32,2,1024]{2,1,0:T(2,128)(2,1)} custom-call(s32[64]{0:T(128)} %reshape.278.need_ref, bf16[32,2,1024]{2,1,0:T(2,128)(2,1)} %maximum_bitcast_fusion.both_ref), custom_call_target="tpu_custom_call" | custom-call | tf_op jit(solution)/shard_map/pallas_call | solution.py:107
  31.9 6.5 %fusion.63 = (bf16[1,3,2048,256]{3,2,1,0:T(8,128)(2,1)}, bf16[1,3,2048,256]{3,2,1,0:T(8,128)(2,1)}, bf16[3,2048,256]{2,1,0:T(8,128)(2,1)}) fusion(bf16[2,3,2048,256]{3,2,1,0:T(8,128)(2,1)} %param.35, s32[]{:T(128)S(6)} %select_n.158), kind=kLoop, calls=%fused_computation.156 | loop fusion | bytes 18874372 | tf_op jit(solution)/shard_map/slice | solution.py:324
  38.4 5.0 %all-to-all-start.2 = ((bf16[32,192,256]{2,1,0:T(8,128)(2,1)}), bf16[32,192,256]{2,1,0:T(8,128)(2,1)}, u32[]{:S(2)}, u32[]{:S(2)}) async-start(bf16[32,192,256]{2,1,0:T(8,128)(2,1)} %bitcast.109), calls=%async_computation.3 | async-start | bytes 6291456 | tf_op jit(solution)/shard_map/all_to_all | solution.py:323
  60.2 21.8 %all-to-all-done.2 = bf16[32,192,256]{2,1,0:T(8,128)(2,1)} async-done(((bf16[32,192,256]{2,1,0:T(8,128)(2,1)}), bf16[32,192,256]{2,1,0:T(8,128)(2,1)}, u32[]{:S(2)}, u32[]{:S(2)}) %all-to-all-start.2) | async-done | bytes 3145760 | tf_op jit(solution)/shard_map/all_to_all | solution.py:323
  82.0 5.1 %all-to-all-start.3 = ((bf16[32,192,256]{2,1,0:T(8,128)(2,1)}), bf16[32,192,256]{2,1,0:T(8,128)(2,1)}, u32[]{:S(2)}, u32[]{:S(2)}) async-start(bf16[32,192,256]{2,1,0:T(8,128)(2,1)} %bitcast.108), calls=%async_computation.4 | async-start | bytes 6291456 | tf_op jit(solution)/shard_map/all_to_all | solution.py:323
  95.2 15.4 %reduce-scatter.2.cloned.1.call-done = f32[64,2048]{1,0:T(8,128)} async-done(((f32[256,2048]{1,0:T(8,128)}), f32[64,2048]{1,0:T(8,128)}) %reduce-scatter.2.cloned.1.call-update) | async-done | bytes 524304 | tf_op jit(solution)/shard_map/reduce_scatter | solution.py:233
  113.1 5.0 %gather_fusion = bf16[1280,16,128]{2,1,0:T(8,128)(2,1)} fusion(bf16[64,16,128]{2,1,0:T(8,128)(2,1)S(1)} %bitcast.105, s32[2048]{0:T(1024)S(1)} %pad_clamp_fusion), kind=kCustom, calls=%fused_computation.2 | custom fusion | bytes 10490880 | tf_op jit(solution)/shard_map/gather | solution.py:288
  118.2 9.4 %bitcast_select_fusion = bf16[128,160,128]{2,1,0:T(8,128)(2,1)} fusion(pred[128,160]{1,0:T(8,128)(4,1)S(1)} %broadcast_in_dim.210, bf16[128,160,128]{2,1,0:T(8,128)(2,1)} %bitcast.106), kind=kLoop, calls=%fused_computation.11 | loop fusion | flops 2621440 | bytes 10506240 | tf_op jit(solution)/shard_map/jit(_where)/select_n | solution.py:287
  127.6 9.6 %all-to-all-done.3 = bf16[32,192,256]{2,1,0:T(8,128)(2,1)} async-done(((bf16[32,192,256]{2,1,0:T(8,128)(2,1)}), bf16[32,192,256]{2,1,0:T(8,128)(2,1)}, u32[]{:S(2)}, u32[]{:S(2)}) %all-to-all-start.3) | async-done | bytes 3145760 | tf_op jit(solution)/shard_map/all_to_all | solution.py:323
  137.2 6.7 %all-to-all-start = ((bf16[128,160,128]{2,1,0:T(8,128)(2,1)}), bf16[128,160,128]{2,1,0:T(8,128)(2,1)}, u32[]{:S(2)}, u32[]{:S(2)}) async-start(bf16[128,160,128]{2,1,0:T(8,128)(2,1)} %bitcast_select_fusion), calls=%async_computation.1 | async-start | bytes 10485760 | tf_op jit(solution)/shard_map/all_to_all | solution.py:291
  145.5 6.1 %pad_maximum_fusion = bf16[32,2,192,256]{3,2,1,0:T(8,128)(2,1)} fusion(bf16[32,1,192,256]{3,2,1,0:T(8,128)(2,1)} %bitcast.34, bf16[32,1,192,256]{3,2,1,0:T(8,128)(2,1)} %bitcast.32), kind=kLoop, calls=%fused_computation.10 | loop fusion | flops 3145728 | bytes 12582912 | tf_op jit(solution)/shard_map/stack | solution.py:332
  151.6 5.2 %gather_fusion.1 = bf16[32,192,256]{2,1,0:T(8,128)(2,1)} fusion(bf16[64,192,256]{2,1,0:T(8,128)(2,1)} %bitcast.107, s32[1024]{0:T(1024)S(1)} %pad_clamp_fusion.1), kind=kCustom, calls=%fused_computation.3 | custom fusion | bytes 6291584 | tf_op jit(solution)/shard_map/jit(_take)/gather | solution.py:337
  156.8 3.9 %broadcast_select_fusion = bf16[32,192,256]{2,1,0:T(8,128)(2,1)} fusion(bf16[32,192,256]{2,1,0:T(8,128)(2,1)} %gather_fusion.1, pred[32]{0:T(512)(128)(4,1)S(1)} %compare_and_fusion.4), kind=kLoop, calls=%fused_computation.15 | loop fusion | flops 1572864 | bytes 6291488 | tf_op jit(solution)/shard_map/jit(_take)/select_n | solution.py:337
  160.7 47.3 %all-to-all-done = bf16[128,160,128]{2,1,0:T(8,128)(2,1)} async-done(((bf16[128,160,128]{2,1,0:T(8,128)(2,1)}), bf16[128,160,128]{2,1,0:T(8,128)(2,1)}, u32[]{:S(2)}, u32[]{:S(2)}) %all-to-all-start) | async-done | bytes 5242912 | tf_op jit(solution)/shard_map/all_to_all | solution.py:291
  208.0 4.8 %all-to-all-start.4 = ((bf16[32,192,256]{2,1,0:T(8,128)(2,1)}), bf16[32,192,256]{2,1,0:T(8,128)(2,1)}, u32[]{:S(2)}, u32[]{:S(2)}) async-start(bf16[32,192,256]{2,1,0:T(8,128)(2,1)} %broadcast_select_fusion), calls=%async_computation.5 | async-start | bytes 6291456 | tf_op jit(solution)/shard_map/all_to_all | solution.py:338
  212.8 8.8 %reshape.287 = bf16[1280,2048]{1,0:T(8,128)(2,1)} reshape(bf16[128,160,128]{2,1,0:T(8,128)(2,1)} %all-to-all-done) | data formatting | bytes 10485760 | tf_op jit(solution)/shard_map/reshape | solution.py:273
  221.7 5.5 %fusion.7 = f32[1280,256]{1,0:T(8,128)} fusion(bf16[1280,2048]{1,0:T(8,128)(2,1)} %reshape.287, bf16[2,3,2048,256]{3,2,1,0:T(8,128)(2,1)} %param.35, s32[]{:T(128)S(6)} %select_n.157), kind=kOutput, calls=%fused_computation.33 | convolution fusion | flops 1342177280 | bytes 7602180 | tf_op jit(solution)/shard_map/dot_general | solution.py:295
  230.0 11.2 %convolution_convert_fusion.1 = bf16[1280,2048]{1,0:T(8,128)(2,1)} fusion(bf16[1280,2048]{1,0:T(8,128)(2,1)} %reshape.287, f32[1280,256]{1,0:T(8,128)} %fusion.7, bf16[2,3,2048,256]{3,2,1,0:T(8,128)(2,1)} %param.35, s32[]{:T(128)S(6)} %select_n.157, s32[]{:T(128)S(6)} %add.207, s32[]{:T(128)S(6)} %add.206), kind=kOutput, calls=%fused_computation.9 | convolution fusion | flops 2688942080 | bytes 13895680 | tf_op jit(solution)/shard_map/dot_general | solution.py:298
  241.2 12.4 %add_convert_fusion = bf16[1280,2048]{1,0:T(8,128)(2,1)} fusion(bf16[1280,2048]{1,0:T(8,128)(2,1)} %convolution_convert_fusion.1, bf16[3,2048,256]{2,1,0:T(8,128)(2,1)} %collective-permute-done, f32[1280,256]{1,0:T(8,128)S(1)} %fusion.6, bf16[1280,2048]{1,0:T(8,128)(2,1)} %reshape.287), kind=kOutput, calls=%fused_computation.7 | convolution fusion | flops 2699427840 | bytes 19136512 | tf_op jit(solution)/shard_map/dot_general | solution.py:298
  253.6 8.9 %reshape.288 = bf16[128,160,128]{2,1,0:T(8,128)(2,1)} reshape(bf16[1280,2048]{1,0:T(8,128)(2,1)} %add_convert_fusion) | data formatting | bytes 10485760 | tf_op jit(solution)/shard_map/reshape | solution.py:270
  262.5 8.7 %all-to-all-start.1 = ((bf16[128,160,128]{2,1,0:T(8,128)(2,1)}), bf16[128,160,128]{2,1,0:T(8,128)(2,1)}, u32[]{:S(2)}, u32[]{:S(2)}) async-start(bf16[128,160,128]{2,1,0:T(8,128)(2,1)} %reshape.288), calls=%async_computation.2 | async-start | bytes 10485760 | tf_op jit(solution)/shard_map/all_to_all | solution.py:303
  271.4 63.8 %all-to-all-done.1 = bf16[128,160,128]{2,1,0:T(8,128)(2,1)} async-done(((bf16[128,160,128]{2,1,0:T(8,128)(2,1)}), bf16[128,160,128]{2,1,0:T(8,128)(2,1)}, u32[]{:S(2)}, u32[]{:S(2)}) %all-to-all-start.1) | async-done | bytes 5242912 | tf_op jit(solution)/shard_map/all_to_all | solution.py:303
  338.9 4.9 %gather_fusion.3 = bf16[512,16,128]{2,1,0:T(8,128)(2,1)} fusion(bf16[1280,16,128]{2,1,0:T(8,128)(2,1)} %bitcast.29, s32[1024]{0:T(1024)S(1)} %get-tuple-element.45), kind=kCustom, calls=%fused_computation.1.clone | custom fusion | bytes 4196352 | tf_op jit(solution)/shard_map/jit(_take)/gather | solution.py:311
  343.7 5.6 %multiply_reduce_fusion = f32[64,16,128]{2,1,0:T(8,128)S(1)} fusion(f32[64,8]{1,0:T(8,128)S(1)} %copy.56, bf16[512,16,128]{2,1,0:T(8,128)(2,1)} %gather_fusion.3, pred[512]{0:T(512)(128)(4,1)S(1)} %get-tuple-element.35, bf16[512,16,128]{2,1,0:T(8,128)(2,1)S(1)} %gather_fusion.2, pred[512]{0:T(512)(128)(4,1)S(1)} %get-tuple-element.16), kind=kLoop, calls=%fused_computation.12 | loop fusion | flops 7208960 | bytes 4721664 | tf_op jit(solution)/shard_map/reduce_sum | solution.py:313
  (122 shorter events, 44.4 us)
Async XLA Ops:
  7.2 50.9 %copy-start = (bf16[512,2048]{1,0:T(8,128)(2,1)S(1)}, bf16[512,2048]{1,0:T(8,128)(2,1)}, u32[]{:S(2)}) copy-start(bf16[512,2048]{1,0:T(8,128)(2,1)} %param.29) | copy-start | bytes 6291460
  38.4 5.9 %copy-start.13 = (s32[1,4]{1,0:T(1,128)S(1)}, s32[1,4]{1,0:T(1,128)}, u32[]{:S(2)}) copy-start(s32[1,4]{1,0:T(1,128)} %param.28) | copy-start | bytes 52
  38.4 7.6 %copy-start.6 = (bf16[256,512]{1,0:T(8,128)(2,1)S(1)}, bf16[256,512]{1,0:T(8,128)(2,1)}, u32[]{:S(2)}) copy-start(bf16[256,512]{1,0:T(8,128)(2,1)} %param.20) | copy-start | bytes 786436
  38.4 7.9 %copy-start.7 = (bf16[256,512]{1,0:T(8,128)(2,1)S(1)}, bf16[256,512]{1,0:T(8,128)(2,1)}, u32[]{:S(2)}) copy-start(bf16[256,512]{1,0:T(8,128)(2,1)} %param.21) | copy-start | bytes 786436
  38.4 43.5 %all-to-all-start.2 = ((bf16[32,192,256]{2,1,0:T(8,128)(2,1)}), bf16[32,192,256]{2,1,0:T(8,128)(2,1)}, u32[]{:S(2)}, u32[]{:S(2)}) async-start(bf16[32,192,256]{2,1,0:T(8,128)(2,1)} %bitcast.109), calls=%async_computation.3 | async-start | bytes 6291456 | tf_op jit(solution)/shard_map/all_to_all | solution.py:323
  43.4 4.5 %copy-start.5 = (bf16[32,2,1024]{2,1,0:T(2,128)(2,1)S(1)}, bf16[32,2,1024]{2,1,0:T(2,128)(2,1)}, u32[]{:S(2)}) copy-start(bf16[32,2,1024]{2,1,0:T(2,128)(2,1)} %shard_map.176) | copy-start | bytes 393220
  43.4 67.3 %reduce-scatter.2.cloned.1.call-start = ((), (), s32[]{:S(2)}) async-start(), calls=%async_computation.6 | async-start | bytes 2621440 | tf_op jit(solution)/shard_map/reduce_scatter | solution.py:233
  49.8 4.2 %copy-start.9 = (pred[256,320]{0,1:T(8,128)(4,1)S(1)}, pred[256,320]{0,1:T(8,128)(4,1)}, u32[]{:S(2)}) copy-start(pred[256,320]{0,1:T(8,128)(4,1)} %broadcast_compare_fusion) | copy-start | bytes 245764
  53.5 2.8 copy-start.8
  82.0 5.2 %copy-start.11 = (s32[64,8]{0,1:T(8,128)S(1)}, s32[64,8]{0,1:T(8,128)}, u32[]{:S(2)}) copy-start(s32[64,8]{0,1:T(8,128)} %param.31) | copy-start | bytes 6148
  82.0 6.9 %copy-start.14 = (s32[64]{0:T(128)S(1)}, s32[64]{0:T(128)}, u32[]{:S(2)}) copy-start(s32[64]{0:T(128)} %param.33) | copy-start | bytes 772
  82.0 28.7 %copy-start.4 = (bf16[64,2048]{1,0:T(8,128)(2,1)S(1)}, bf16[64,2048]{1,0:T(8,128)(2,1)}, u32[]{:S(2)}) copy-start(bf16[64,2048]{1,0:T(8,128)(2,1)} %param.19) | copy-start | bytes 786436
  82.0 29.9 %copy-start.10 = (f32[2048]{0:T(1024)S(1)}, f32[2048]{0:T(1024)}, u32[]{:S(2)}) copy-start(f32[2048]{0:T(1024)} %param.30) | copy-start | bytes 24580
  82.0 55.2 %all-to-all-start.3 = ((bf16[32,192,256]{2,1,0:T(8,128)(2,1)}), bf16[32,192,256]{2,1,0:T(8,128)(2,1)}, u32[]{:S(2)}, u32[]{:S(2)}) async-start(bf16[32,192,256]{2,1,0:T(8,128)(2,1)} %bitcast.108), calls=%async_computation.4 | async-start | bytes 6291456 | tf_op jit(solution)/shard_map/all_to_all | solution.py:323
  127.6 17.7 %copy-start.15 = (s32[32]{0:T(128)S(1)}, s32[32]{0:T(128)}, u32[]{:S(2)}) copy-start(s32[32]{0:T(128)} %param.34) | copy-start | bytes 388
  137.2 70.8 %all-to-all-start = ((bf16[128,160,128]{2,1,0:T(8,128)(2,1)}), bf16[128,160,128]{2,1,0:T(8,128)(2,1)}, u32[]{:S(2)}, u32[]{:S(2)}) async-start(bf16[128,160,128]{2,1,0:T(8,128)(2,1)} %bitcast_select_fusion), calls=%async_computation.1 | async-start | bytes 10485760 | tf_op jit(solution)/shard_map/all_to_all | solution.py:291
  143.9 83.3 %collective-permute-start = (bf16[3,2048,256]{2,1,0:T(8,128)(2,1)}, bf16[3,2048,256]{2,1,0:T(8,128)(2,1)}, u32[]{:S(2)}, u32[]{:S(2)}) collective-permute-start(bf16[3,2048,256]{2,1,0:T(8,128)(2,1)} %get-tuple-element.24), channel_id=1, source_target_pairs={{0,1},{1,0},{2,3},{3,2},{4,5},{5,4},{6,7},{7,6},{8,9},{9,8},{10,11... | collective-permute-start | bytes 9437192 | tf_op jit(solution)/shard_map/ppermute | solution.py:265
  208.0 54.5 %all-to-all-start.4 = ((bf16[32,192,256]{2,1,0:T(8,128)(2,1)}), bf16[32,192,256]{2,1,0:T(8,128)(2,1)}, u32[]{:S(2)}, u32[]{:S(2)}) async-start(bf16[32,192,256]{2,1,0:T(8,128)(2,1)} %broadcast_select_fusion), calls=%async_computation.5 | async-start | bytes 6291456 | tf_op jit(solution)/shard_map/all_to_all | solution.py:338
  221.7 5.5 %copy-start.2 = (bf16[1280,2048]{1,0:T(8,128)(2,1)S(1)}, bf16[1280,2048]{1,0:T(8,128)(2,1)}, u32[]{:S(2)}) copy-start(bf16[1280,2048]{1,0:T(8,128)(2,1)} %reshape.287) | copy-start | bytes 15728644
  262.5 8.7 %copy-start.12 = (f32[64,8]{0,1:T(8,128)S(1)}, f32[64,8]{0,1:T(8,128)}, u32[]{:S(2)}) copy-start(f32[64,8]{0,1:T(8,128)} %param.32) | copy-start | bytes 6148
  262.5 72.7 %all-to-all-start.1 = ((bf16[128,160,128]{2,1,0:T(8,128)(2,1)}), bf16[128,160,128]{2,1,0:T(8,128)(2,1)}, u32[]{:S(2)}, u32[]{:S(2)}) async-start(bf16[128,160,128]{2,1,0:T(8,128)(2,1)} %reshape.288), calls=%async_computation.2 | async-start | bytes 10485760 | tf_op jit(solution)/shard_map/all_to_all | solution.py:303
  343.7 5.6 %copy-start.3 = (f32[64,2048]{1,0:T(8,128)S(1)}, f32[64,2048]{1,0:T(8,128)}, u32[]{:S(2)}) copy-start(f32[64,2048]{1,0:T(8,128)} %reduce-scatter.2.cloned.1.call-done) | copy-start | bytes 1572868
  349.3 4.7 %copy-start.1 = (bf16[512,2048]{1,0:T(8,128)(2,1)S(1)}, bf16[512,2048]{1,0:T(8,128)(2,1)}, u32[]{:S(2)}) copy-start(bf16[512,2048]{1,0:T(8,128)(2,1)} %param.29) | copy-start | bytes 6291460
Sparse Core Ops, SparseCore 0:
  60.3 50.3 reduce-scatter.1

commit v3 on v2

--- a/solution.py
+++ b/solution.py
@@ -288,6 +288,7 @@
         copy_filled[..., None, None], normed_tiles[copy_token], jnp.bfloat16(0)
     )
     copies = copies.reshape(req_count * exp_count, tile_rows, lanes)
+    got_part, copies = lax.optimization_barrier((got_part, copies))
     inbox = lax.all_to_all(copies, ("req", "exp"), split_axis=0, concat_axis=0, tiled=True)
     in_rows = as_rows(inbox)
     halves = []

time: 363 us -> 363 us (level)
  transfers between devices with their start and end apart: 7 -> 7, of which waited for: 5 -> 5; matrix products, arithmetic and copies ran while one was open for 30% -> 29% of each run, Pallas kernels for 0% -> 0%
where the time goes in v3:
time: 363 us; the launch traced here: 361 us
  waiting for transfers between devices  157 us (43%)
  local copies, waits for them, and re-layouts  59.5 us (16%)
  matrix products  38.9 us (11%)
  other arithmetic  37.8 us (10%)
  starting transfers between devices  33.2 us (9%)
  Pallas kernels  20.2 us (6%)
  between operations  14.6 us (4%)
    all_to_all x1, waiting for transfers between devices, body(): lax.all_to_all(partial_value, ('req', 'exp'), split_axis=0, concat_axis=0...  63.8 us
    all_to_all x1, waiting for transfers between devices, body(): lax.all_to_all(copies, ('req', 'exp'), split_axis=0, concat_axis=0, tiled...  48.6 us
    all_to_all x2, waiting for transfers between devices, body(): lax.all_to_all(slot_weights[c].reshape(req_count, piece_rows, slot_weight...  29.5 us
    dot_general x2, matrix products, body(): lax.dot_general(hidden, part[2], (((1,), (1,)), ((), ())), preferred_elem...  23.6 us
    pallas_call x1, Pallas kernels, exchange_cache(): pl.pallas_call(functools.partial(cache_kernel, n), out_shape=jax.ShapeDty...  20.2 us
    reduce_scatter x1, waiting for transfers between devices, body(): lax.psum_scatter(jnp.dot(attended, out_proj, preferred_element_type=jnp.f...  15 us
    all_to_all x2, starting transfers between devices, body(): lax.all_to_all(slot_weights[c].reshape(req_count, piece_rows, slot_weight...  10.1 us
    select_n x1, other arithmetic, body(): jnp.where(copy_filled[..., None, None], normed_tiles[copy_token], jnp.bfl...  9.43 us
  transfers between devices with their start and end apart: 7, of which 5 were waited for; matrix products, arithmetic and copies ran while one was open for 29% of the time, Pallas kernels for 0%

profile of v3, /device:TPU:1, one launch (start us, length us, event | category | flops | bytes accessed | tf_op | source)
XLA Modules:
  0.0 361.0 jit_solution(10698494602301508170)
XLA Ops:
  11.8 20.2 %shard_map.176 = bf16[32,2,1024]{2,1,0:T(2,128)(2,1)} custom-call(s32[64]{0:T(128)} %reshape.278.need_ref, bf16[32,2,1024]{2,1,0:T(2,128)(2,1)} %maximum_bitcast_fusion.both_ref), custom_call_target="tpu_custom_call" | custom-call | tf_op jit(solution)/shard_map/pallas_call | solution.py:107
  32.0 6.4 %fusion.70 = (bf16[1,3,2048,256]{3,2,1,0:T(8,128)(2,1)}, bf16[1,3,2048,256]{3,2,1,0:T(8,128)(2,1)}, bf16[3,2048,256]{2,1,0:T(8,128)(2,1)}) fusion(bf16[2,3,2048,256]{3,2,1,0:T(8,128)(2,1)} %param.35, s32[]{:T(128)S(6)} %select_n.150), kind=kLoop, calls=%fused_computation.158 | loop fusion | bytes 18874372 | tf_op jit(solution)/shard_map/slice | solution.py:325
  38.4 5.0 %all-to-all-start.3 = ((bf16[32,192,256]{2,1,0:T(8,128)(2,1)}), bf16[32,192,256]{2,1,0:T(8,128)(2,1)}, u32[]{:S(2)}, u32[]{:S(2)}) async-start(bf16[32,192,256]{2,1,0:T(8,128)(2,1)} %bitcast.109), calls=%async_computation.4 | async-start | bytes 6291456 | tf_op jit(solution)/shard_map/all_to_all | solution.py:324
  62.7 19.2 %all-to-all-done.3 = bf16[32,192,256]{2,1,0:T(8,128)(2,1)} async-done(((bf16[32,192,256]{2,1,0:T(8,128)(2,1)}), bf16[32,192,256]{2,1,0:T(8,128)(2,1)}, u32[]{:S(2)}, u32[]{:S(2)}) %all-to-all-start.3) | async-done | bytes 3145760 | tf_op jit(solution)/shard_map/all_to_all | solution.py:324
  81.9 5.1 %all-to-all-start.2 = ((bf16[32,192,256]{2,1,0:T(8,128)(2,1)}), bf16[32,192,256]{2,1,0:T(8,128)(2,1)}, u32[]{:S(2)}, u32[]{:S(2)}) async-start(bf16[32,192,256]{2,1,0:T(8,128)(2,1)} %bitcast.108), calls=%async_computation.3 | async-start | bytes 6291456 | tf_op jit(solution)/shard_map/all_to_all | solution.py:324
  95.2 15.0 %reduce-scatter.2.cloned.1.call-done = f32[64,2048]{1,0:T(8,128)} async-done(((f32[256,2048]{1,0:T(8,128)}), f32[64,2048]{1,0:T(8,128)}) %reduce-scatter.2.cloned.1.call-update) | async-done | bytes 524304 | tf_op jit(solution)/shard_map/reduce_scatter | solution.py:233
  112.6 5.0 %gather_fusion = bf16[1280,16,128]{2,1,0:T(8,128)(2,1)} fusion(bf16[64,16,128]{2,1,0:T(8,128)(2,1)S(1)} %bitcast.105, s32[2048]{0:T(1024)S(1)} %pad_clamp_fusion), kind=kCustom, calls=%fused_computation.2 | custom fusion | bytes 10490880 | tf_op jit(solution)/shard_map/gather | solution.py:288
  117.6 9.4 %bitcast_select_fusion = bf16[128,160,128]{2,1,0:T(8,128)(2,1)} fusion(pred[128,160]{1,0:T(8,128)(4,1)S(1)} %broadcast_in_dim.210, bf16[128,160,128]{2,1,0:T(8,128)(2,1)} %bitcast.106), kind=kLoop, calls=%fused_computation.11 | loop fusion | flops 2621440 | bytes 10506240 | tf_op jit(solution)/shard_map/jit(_where)/select_n | solution.py:287
  127.1 10.3 %all-to-all-done.2 = bf16[32,192,256]{2,1,0:T(8,128)(2,1)} async-done(((bf16[32,192,256]{2,1,0:T(8,128)(2,1)}), bf16[32,192,256]{2,1,0:T(8,128)(2,1)}, u32[]{:S(2)}, u32[]{:S(2)}) %all-to-all-start.2) | async-done | bytes 3145760 | tf_op jit(solution)/shard_map/all_to_all | solution.py:324
  137.4 6.7 %all-to-all-start = ((bf16[128,160,128]{2,1,0:T(8,128)(2,1)}), bf16[128,160,128]{2,1,0:T(8,128)(2,1)}, u32[]{:S(2)}, u32[]{:S(2)}) async-start(bf16[128,160,128]{2,1,0:T(8,128)(2,1)} %bitcast_select_fusion), calls=%async_computation.1 | async-start | bytes 10485760 | tf_op jit(solution)/shard_map/all_to_all | solution.py:292
  144.3 6.1 %pad_maximum_fusion = bf16[32,2,192,256]{3,2,1,0:T(8,128)(2,1)} fusion(bf16[32,1,192,256]{3,2,1,0:T(8,128)(2,1)} %bitcast.34, bf16[32,1,192,256]{3,2,1,0:T(8,128)(2,1)} %bitcast.32), kind=kLoop, calls=%fused_computation.10 | loop fusion | flops 3145728 | bytes 12582912 | tf_op jit(solution)/shard_map/stack | solution.py:333
  150.4 5.2 %gather_fusion.1 = bf16[32,192,256]{2,1,0:T(8,128)(2,1)} fusion(bf16[64,192,256]{2,1,0:T(8,128)(2,1)} %bitcast.107, s32[1024]{0:T(1024)S(1)} %pad_clamp_fusion.1), kind=kCustom, calls=%fused_computation.3 | custom fusion | bytes 6291584 | tf_op jit(solution)/shard_map/jit(_take)/gather | solution.py:338
  155.6 3.9 %broadcast_select_fusion = bf16[32,192,256]{2,1,0:T(8,128)(2,1)} fusion(bf16[32,192,256]{2,1,0:T(8,128)(2,1)} %gather_fusion.1, pred[32]{0:T(512)(128)(4,1)S(1)} %compare_and_fusion.4), kind=kLoop, calls=%fused_computation.15 | loop fusion | flops 1572864 | bytes 6291488 | tf_op jit(solution)/shard_map/jit(_take)/select_n | solution.py:338
  159.5 48.6 %all-to-all-done = bf16[128,160,128]{2,1,0:T(8,128)(2,1)} async-done(((bf16[128,160,128]{2,1,0:T(8,128)(2,1)}), bf16[128,160,128]{2,1,0:T(8,128)(2,1)}, u32[]{:S(2)}, u32[]{:S(2)}) %all-to-all-start) | async-done | bytes 5242912 | tf_op jit(solution)/shard_map/all_to_all | solution.py:292
  208.2 4.8 %all-to-all-start.4 = ((bf16[32,192,256]{2,1,0:T(8,128)(2,1)}), bf16[32,192,256]{2,1,0:T(8,128)(2,1)}, u32[]{:S(2)}, u32[]{:S(2)}) async-start(bf16[32,192,256]{2,1,0:T(8,128)(2,1)} %broadcast_select_fusion), calls=%async_computation.5 | async-start | bytes 6291456 | tf_op jit(solution)/shard_map/all_to_all | solution.py:339
  213.0 8.8 %reshape.287 = bf16[1280,2048]{1,0:T(8,128)(2,1)} reshape(bf16[128,160,128]{2,1,0:T(8,128)(2,1)} %all-to-all-done) | data formatting | bytes 10485760 | tf_op jit(solution)/shard_map/reshape | solution.py:273
  221.8 5.5 %fusion.6 = f32[1280,256]{1,0:T(8,128)} fusion(bf16[1280,2048]{1,0:T(8,128)(2,1)} %reshape.287, bf16[2,3,2048,256]{3,2,1,0:T(8,128)(2,1)} %param.35, s32[]{:T(128)S(6)} %select_n.158), kind=kOutput, calls=%fused_computation.29 | convolution fusion | flops 1342177280 | bytes 7602180 | tf_op jit(solution)/shard_map/dot_general | solution.py:296
  230.2 10.8 %convolution_convert_fusion = bf16[1280,2048]{1,0:T(8,128)(2,1)} fusion(bf16[1280,2048]{1,0:T(8,128)(2,1)} %reshape.287, f32[1280,256]{1,0:T(8,128)S(1)} %fusion.10, bf16[3,2048,256]{2,1,0:T(8,128)(2,1)} %collective-permute-done), kind=kOutput, calls=%fused_computation.8 | convolution fusion | flops 2688942080 | bytes 13893632 | tf_op jit(solution)/shard_map/dot_general | solution.py:299
  241.0 12.8 %add_convert_fusion = bf16[1280,2048]{1,0:T(8,128)(2,1)} fusion(bf16[1280,2048]{1,0:T(8,128)(2,1)} %convolution_convert_fusion, bf16[2,3,2048,256]{3,2,1,0:T(8,128)(2,1)} %param.35, s32[]{:T(128)S(6)} %select_n.158, s32[]{:T(128)S(6)} %add.207, bf16[1280,2048]{1,0:T(8,128)(2,1)} %reshape.287, f32[1280,256]{1,0:T(8,128)} %fusion.6, s32[]{:T(128)S(6)} %add.206), kind=kOutput, calls=%fused_computation.7 | convolution fusion | flops 2699427840 | bytes 19138560 | tf_op jit(solution)/shard_map/dot_general | solution.py:299
  253.7 8.9 %reshape.288 = bf16[128,160,128]{2,1,0:T(8,128)(2,1)} reshape(bf16[1280,2048]{1,0:T(8,128)(2,1)} %add_convert_fusion) | data formatting | bytes 10485760 | tf_op jit(solution)/shard_map/reshape | solution.py:270
  262.7 8.7 %all-to-all-start.1 = ((bf16[128,160,128]{2,1,0:T(8,128)(2,1)}), bf16[128,160,128]{2,1,0:T(8,128)(2,1)}, u32[]{:S(2)}, u32[]{:S(2)}) async-start(bf16[128,160,128]{2,1,0:T(8,128)(2,1)} %reshape.288), calls=%async_computation.2 | async-start | bytes 10485760 | tf_op jit(solution)/shard_map/all_to_all | solution.py:304
  271.5 63.8 %all-to-all-done.1 = bf16[128,160,128]{2,1,0:T(8,128)(2,1)} async-done(((bf16[128,160,128]{2,1,0:T(8,128)(2,1)}), bf16[128,160,128]{2,1,0:T(8,128)(2,1)}, u32[]{:S(2)}, u32[]{:S(2)}) %all-to-all-start.1) | async-done | bytes 5242912 | tf_op jit(solution)/shard_map/all_to_all | solution.py:304
  339.0 4.9 %gather_fusion.2 = bf16[512,16,128]{2,1,0:T(8,128)(2,1)} fusion(bf16[1280,16,128]{2,1,0:T(8,128)(2,1)} %bitcast.29, s32[1024]{0:T(1024)S(1)} %get-tuple-element.50), kind=kCustom, calls=%fused_computation.clone | custom fusion | bytes 4196352 | tf_op jit(solution)/shard_map/jit(_take)/gather | solution.py:312
  343.9 5.5 %multiply_reduce_fusion = f32[64,16,128]{2,1,0:T(8,128)S(1)} fusion(f32[64,8]{1,0:T(8,128)S(1)} %copy.56, bf16[512,16,128]{2,1,0:T(8,128)(2,1)S(1)} %gather_fusion.3, pred[512]{0:T(512)(128)(4,1)S(1)} %get-tuple-element.39, bf16[512,16,128]{2,1,0:T(8,128)(2,1)} %gather_fusion.2, pred[512]{0:T(512)(128)(4,1)S(1)} %get-tuple-element.20), kind=kLoop, calls=%fused_computation.12 | loop fusion | flops 7208960 | bytes 4721664 | tf_op jit(solution)/shard_map/reduce_sum | solution.py:314
  (120 shorter events, 45.7 us)
Async XLA Ops:
  7.2 50.7 %copy-start = (bf16[512,2048]{1,0:T(8,128)(2,1)S(1)}, bf16[512,2048]{1,0:T(8,128)(2,1)}, u32[]{:S(2)}) copy-start(bf16[512,2048]{1,0:T(8,128)(2,1)} %param.29) | copy-start | bytes 6291460
  38.4 5.6 %copy-start.12 = (s32[1,4]{1,0:T(1,128)S(1)}, s32[1,4]{1,0:T(1,128)}, u32[]{:S(2)}) copy-start(s32[1,4]{1,0:T(1,128)} %param.28) | copy-start | bytes 52
  38.4 6.2 %copy-start.5 = (bf16[32,2,1024]{2,1,0:T(2,128)(2,1)S(1)}, bf16[32,2,1024]{2,1,0:T(2,128)(2,1)}, u32[]{:S(2)}) copy-start(bf16[32,2,1024]{2,1,0:T(2,128)(2,1)} %shard_map.176) | copy-start | bytes 393220
  38.4 7.8 %copy-start.6 = (bf16[256,512]{1,0:T(8,128)(2,1)S(1)}, bf16[256,512]{1,0:T(8,128)(2,1)}, u32[]{:S(2)}) copy-start(bf16[256,512]{1,0:T(8,128)(2,1)} %param.20) | copy-start | bytes 786436
  38.4 8.6 %copy-start.7 = (bf16[256,512]{1,0:T(8,128)(2,1)S(1)}, bf16[256,512]{1,0:T(8,128)(2,1)}, u32[]{:S(2)}) copy-start(bf16[256,512]{1,0:T(8,128)(2,1)} %param.21) | copy-start | bytes 786436
  38.4 9.4 %copy-start.8 = (bf16[256,512]{1,0:T(8,128)(2,1)S(1)}, bf16[256,512]{1,0:T(8,128)(2,1)}, u32[]{:S(2)}) copy-start(bf16[256,512]{1,0:T(8,128)(2,1)} %param.22) | copy-start | bytes 786436
  38.4 43.5 %all-to-all-start.3 = ((bf16[32,192,256]{2,1,0:T(8,128)(2,1)}), bf16[32,192,256]{2,1,0:T(8,128)(2,1)}, u32[]{:S(2)}, u32[]{:S(2)}) async-start(bf16[32,192,256]{2,1,0:T(8,128)(2,1)} %bitcast.109), calls=%async_computation.4 | async-start | bytes 6291456 | tf_op jit(solution)/shard_map/all_to_all | solution.py:324
  43.4 66.8 %reduce-scatter.2.cloned.1.call-start = ((), (), s32[]{:S(2)}) async-start(), calls=%async_computation.6 | async-start | bytes 2621440 | tf_op jit(solution)/shard_map/reduce_scatter | solution.py:233
  59.9 67.1 %collective-permute-start = (bf16[3,2048,256]{2,1,0:T(8,128)(2,1)}, bf16[3,2048,256]{2,1,0:T(8,128)(2,1)}, u32[]{:S(2)}, u32[]{:S(2)}) collective-permute-start(bf16[3,2048,256]{2,1,0:T(8,128)(2,1)} %get-tuple-element.28), channel_id=1, source_target_pairs={{0,1},{1,0},{2,3},{3,2},{4,5},{5,4},{6,7},{7,6},{8,9},{9,8},{10,11... | collective-permute-start | bytes 9437192 | tf_op jit(solution)/shard_map/ppermute | solution.py:265
  81.9 5.2 %copy-start.10 = (s32[64,8]{0,1:T(8,128)S(1)}, s32[64,8]{0,1:T(8,128)}, u32[]{:S(2)}) copy-start(s32[64,8]{0,1:T(8,128)} %param.31) | copy-start | bytes 6148
  81.9 6.9 %copy-start.13 = (s32[64]{0:T(128)S(1)}, s32[64]{0:T(128)}, u32[]{:S(2)}) copy-start(s32[64]{0:T(128)} %param.33) | copy-start | bytes 772
  81.9 28.2 %copy-start.4 = (bf16[64,2048]{1,0:T(8,128)(2,1)S(1)}, bf16[64,2048]{1,0:T(8,128)(2,1)}, u32[]{:S(2)}) copy-start(bf16[64,2048]{1,0:T(8,128)(2,1)} %param.19) | copy-start | bytes 786436
  81.9 29.5 %copy-start.9 = (f32[2048]{0:T(1024)S(1)}, f32[2048]{0:T(1024)}, u32[]{:S(2)}) copy-start(f32[2048]{0:T(1024)} %param.30) | copy-start | bytes 24580
  81.9 55.4 %all-to-all-start.2 = ((bf16[32,192,256]{2,1,0:T(8,128)(2,1)}), bf16[32,192,256]{2,1,0:T(8,128)(2,1)}, u32[]{:S(2)}, u32[]{:S(2)}) async-start(bf16[32,192,256]{2,1,0:T(8,128)(2,1)} %bitcast.108), calls=%async_computation.3 | async-start | bytes 6291456 | tf_op jit(solution)/shard_map/all_to_all | solution.py:324
  127.1 17.0 %copy-start.14 = (s32[32]{0:T(128)S(1)}, s32[32]{0:T(128)}, u32[]{:S(2)}) copy-start(s32[32]{0:T(128)} %param.34) | copy-start | bytes 388
  137.4 70.8 %all-to-all-start = ((bf16[128,160,128]{2,1,0:T(8,128)(2,1)}), bf16[128,160,128]{2,1,0:T(8,128)(2,1)}, u32[]{:S(2)}, u32[]{:S(2)}) async-start(bf16[128,160,128]{2,1,0:T(8,128)(2,1)} %bitcast_select_fusion), calls=%async_computation.1 | async-start | bytes 10485760 | tf_op jit(solution)/shard_map/all_to_all | solution.py:292
  208.2 54.5 %all-to-all-start.4 = ((bf16[32,192,256]{2,1,0:T(8,128)(2,1)}), bf16[32,192,256]{2,1,0:T(8,128)(2,1)}, u32[]{:S(2)}, u32[]{:S(2)}) async-start(bf16[32,192,256]{2,1,0:T(8,128)(2,1)} %broadcast_select_fusion), calls=%async_computation.5 | async-start | bytes 6291456 | tf_op jit(solution)/shard_map/all_to_all | solution.py:339
  221.8 5.5 %copy-start.2 = (bf16[1280,2048]{1,0:T(8,128)(2,1)S(1)}, bf16[1280,2048]{1,0:T(8,128)(2,1)}, u32[]{:S(2)}) copy-start(bf16[1280,2048]{1,0:T(8,128)(2,1)} %reshape.287) | copy-start | bytes 15728644
  262.7 8.7 %copy-start.11 = (f32[64,8]{0,1:T(8,128)S(1)}, f32[64,8]{0,1:T(8,128)}, u32[]{:S(2)}) copy-start(f32[64,8]{0,1:T(8,128)} %param.32) | copy-start | bytes 6148
  262.7 72.7 %all-to-all-start.1 = ((bf16[128,160,128]{2,1,0:T(8,128)(2,1)}), bf16[128,160,128]{2,1,0:T(8,128)(2,1)}, u32[]{:S(2)}, u32[]{:S(2)}) async-start(bf16[128,160,128]{2,1,0:T(8,128)(2,1)} %reshape.288), calls=%async_computation.2 | async-start | bytes 10485760 | tf_op jit(solution)/shard_map/all_to_all | solution.py:304
  343.9 5.6 %copy-start.3 = (f32[64,2048]{1,0:T(8,128)S(1)}, f32[64,2048]{1,0:T(8,128)}, u32[]{:S(2)}) copy-start(f32[64,2048]{1,0:T(8,128)} %reduce-scatter.2.cloned.1.call-done) | copy-start | bytes 1572868
  349.5 4.7 %copy-start.1 = (bf16[512,2048]{1,0:T(8,128)(2,1)S(1)}, bf16[512,2048]{1,0:T(8,128)(2,1)}, u32[]{:S(2)}) copy-start(bf16[512,2048]{1,0:T(8,128)(2,1)} %param.29) | copy-start | bytes 6291460
Sparse Core Ops, SparseCore 0:
  60.1 50.0 reduce-scatter.1

commit v4 on v2

--- a/solution.py
+++ b/solution.py
@@ -260,7 +260,23 @@
     pair_bit = exp_idx % 2
     pair_count = exp_count // 2
     own_part = lax.dynamic_index_in_dim(slot_weights, pair_bit, 0, keepdims=False)
-    give_part = lax.dynamic_index_in_dim(slot_weights, 1 - pair_bit, 0, keepdims=False)
+    stacked_rows = slot_weights.shape[1] * slot_weights.shape[2]
+    piece_rows = stacked_rows // req_count
+
+    def spread_slot(weights, c):
+        return lax.all_to_all(
+            weights[c].reshape(req_count, piece_rows, slot_weights.shape[3]),
+            "req",
+            split_axis=0,
+            concat_axis=0,
+            tiled=True,
+        )
+
+    first_spread = spread_slot(slot_weights, 0)
+    late_weights, first_spread = lax.optimization_barrier((slot_weights, first_spread))
+    spread = [first_spread] + [spread_slot(late_weights, c) for c in range(1, slots_here)]
+    swap_weights, spread = lax.optimization_barrier((slot_weights, spread))
+    give_part = lax.dynamic_index_in_dim(swap_weights, 1 - pair_bit, 0, keepdims=False)
     swap = [(e, e ^ 1) for e in range(exp_count)]
     got_part = lax.ppermute(give_part, "exp", perm=swap)
     lanes = 128
@@ -317,18 +333,6 @@
     )
     residual_tiles = residual.reshape(tok_dev, tile_high, lanes)
     layer_out = (residual_tiles + mixture).astype(jnp.bfloat16).reshape(tok_dev, model_width)
-    stacked_rows = slot_weights.shape[1] * slot_weights.shape[2]
-    piece_rows = stacked_rows // req_count
-    spread = [
-        lax.all_to_all(
-            slot_weights[c].reshape(req_count, piece_rows, slot_weights.shape[3]),
-            "req",
-            split_axis=0,
-            concat_axis=0,
-            tiled=True,
-        )
-        for c in range(slots_here)
-    ]
     spread_slots = jnp.stack(spread, axis=1).reshape(
         slot_total, piece_rows, slot_weights.shape[3]
     )

time: 363 us -> 362 us (level)
  waiting for transfers between devices: 158 us -> 151 us
  local copies, waits for them, and re-layouts: 60.4 us -> 64.4 us
    reduce_scatter x1, waiting for transfers between devices: 15.4 us -> 6.95 us  [body(): lax.psum_scatter(jnp.dot(attended, out_proj, preferred_element_type=jnp.f...]
    all_to_all x2, waiting for transfers between devices: 31.4 us -> 36.8 us  [spread_slot(): lax.all_to_all(weights[c].reshape(req_count, piece_rows, slot_weights.sha...]
    squeeze x0 -> x1, local copies, waits for them, and re-layouts: none -> 3.76 us  [body(): lax.dynamic_index_in_dim(swap_weights, 1 - pair_bit, 0, keepdims=False)]
    all_to_all x1, waiting for transfers between devices: 47.3 us -> 43.6 us  [body(): lax.all_to_all(copies, ('req', 'exp'), split_axis=0, concat_axis=0, tiled...]
    slice x2 -> x3, local copies, waits for them, and re-layouts: 6.7 us -> 7.74 us  [the longest x2 7.51 us: spread_slot(): weights[c].reshape(req_count, piece_rows, slot_weights.shape[3])]
  transfers between devices with their start and end apart: 7 -> 7, of which waited for: 5 -> 5; matrix products, arithmetic and copies ran while one was open for 30% -> 32% of each run, Pallas kernels for 0% -> 0%
where the time goes in v4:
time: 362 us; the launch traced here: 360 us
  waiting for transfers between devices  151 us (42%)
  local copies, waits for them, and re-layouts  64.4 us (18%)
  matrix products  38.9 us (11%)
  other arithmetic  37.6 us (10%)
  starting transfers between devices  33.6 us (9%)
  Pallas kernels  20.2 us (6%)
  between operations  14.5 us (4%)
    all_to_all x1, waiting for transfers between devices, body(): lax.all_to_all(partial_value, ('req', 'exp'), split_axis=0, concat_axis=0...  63.8 us
    all_to_all x1, waiting for transfers between devices, body(): lax.all_to_all(copies, ('req', 'exp'), split_axis=0, concat_axis=0, tiled...  43.6 us
    all_to_all x2, waiting for transfers between devices, spread_slot(): lax.all_to_all(weights[c].reshape(req_count, piece_rows, slot_weights.sha...  36.8 us
    dot_general x2, matrix products, body(): lax.dot_general(hidden, part[2], (((1,), (1,)), ((), ())), preferred_elem...  23.6 us
    pallas_call x1, Pallas kernels, exchange_cache(): pl.pallas_call(functools.partial(cache_kernel, n), out_shape=jax.ShapeDty...  20.2 us
    all_to_all x2, starting transfers between devices, spread_slot(): lax.all_to_all(weights[c].reshape(req_count, piece_rows, slot_weights.sha...  10.1 us
    select_n x1, other arithmetic, body(): jnp.where(copy_filled[..., None, None], normed_tiles[copy_token], jnp.bfl...  9.43 us
    reshape x1, local copies, waits for them, and re-layouts, as_tiles(): return rows.reshape(req_count * exp_count, tile_rows, lanes)  8.93 us
  transfers between devices with their start and end apart: 7, of which 5 were waited for; matrix products, arithmetic and copies ran while one was open for 32% of the time, Pallas kernels for 0%

profile of v4, /device:TPU:1, one launch (start us, length us, event | category | flops | bytes accessed | tf_op | source)
XLA Modules:
  0.0 360.3 jit_solution(8157141866257065046)
XLA Ops:
  11.8 20.2 %shard_map.176 = bf16[32,2,1024]{2,1,0:T(2,128)(2,1)} custom-call(s32[64]{0:T(128)} %reshape.278.need_ref, bf16[32,2,1024]{2,1,0:T(2,128)(2,1)} %maximum_bitcast_fusion.both_ref), custom_call_target="tpu_custom_call" | custom-call | tf_op jit(solution)/shard_map/pallas_call | solution.py:107
  35.7 5.0 %all-to-all-start.1 = ((bf16[32,192,256]{2,1,0:T(8,128)(2,1)}), bf16[32,192,256]{2,1,0:T(8,128)(2,1)}, u32[]{:S(2)}, u32[]{:S(2)}) async-start(bf16[32,192,256]{2,1,0:T(8,128)(2,1)} %bitcast.110), calls=%async_computation.2 | async-start | bytes 6291456 | tf_op jit(solution)/shard_map/all_to_all | solution.py:267
  57.1 22.1 %all-to-all-done.1 = bf16[32,192,256]{2,1,0:T(8,128)(2,1)} async-done(((bf16[32,192,256]{2,1,0:T(8,128)(2,1)}), bf16[32,192,256]{2,1,0:T(8,128)(2,1)}, u32[]{:S(2)}, u32[]{:S(2)}) %all-to-all-start.1) | async-done | bytes 3145760 | tf_op jit(solution)/shard_map/all_to_all | solution.py:267
  83.0 5.1 %all-to-all-start.2 = ((bf16[32,192,256]{2,1,0:T(8,128)(2,1)}), bf16[32,192,256]{2,1,0:T(8,128)(2,1)}, u32[]{:S(2)}, u32[]{:S(2)}) async-start(bf16[32,192,256]{2,1,0:T(8,128)(2,1)} %bitcast.111), calls=%async_computation.3 | async-start | bytes 6291456 | tf_op jit(solution)/shard_map/all_to_all | solution.py:267
  96.3 6.9 %reduce-scatter.2.cloned.1.call-done = f32[64,2048]{1,0:T(8,128)} async-done(((f32[256,2048]{1,0:T(8,128)}), f32[64,2048]{1,0:T(8,128)}) %reduce-scatter.2.cloned.1.call-update) | async-done | bytes 524304 | tf_op jit(solution)/shard_map/reduce_scatter | solution.py:233
  105.7 5.0 %gather_fusion = bf16[1280,16,128]{2,1,0:T(8,128)(2,1)} fusion(bf16[64,16,128]{2,1,0:T(8,128)(2,1)S(1)} %bitcast.107, s32[2048]{0:T(1024)S(1)} %pad_clamp_fusion), kind=kCustom, calls=%fused_computation.2 | custom fusion | bytes 10490880 | tf_op jit(solution)/shard_map/gather | solution.py:304
  110.7 9.4 %bitcast_select_fusion = bf16[128,160,128]{2,1,0:T(8,128)(2,1)} fusion(pred[128,160]{1,0:T(8,128)(4,1)S(1)} %broadcast_in_dim.210, bf16[128,160,128]{2,1,0:T(8,128)(2,1)} %bitcast.108), kind=kLoop, calls=%fused_computation.11 | loop fusion | flops 2621440 | bytes 10506240 | tf_op jit(solution)/shard_map/jit(_where)/select_n | solution.py:303
  120.1 14.7 %all-to-all-done.2 = bf16[32,192,256]{2,1,0:T(8,128)(2,1)} async-done(((bf16[32,192,256]{2,1,0:T(8,128)(2,1)}), bf16[32,192,256]{2,1,0:T(8,128)(2,1)}, u32[]{:S(2)}, u32[]{:S(2)}) %all-to-all-start.2) | async-done | bytes 3145760 | tf_op jit(solution)/shard_map/all_to_all | solution.py:267
  134.8 8.8 %all-to-all-start = ((bf16[128,160,128]{2,1,0:T(8,128)(2,1)}), bf16[128,160,128]{2,1,0:T(8,128)(2,1)}, u32[]{:S(2)}, u32[]{:S(2)}) async-start(bf16[128,160,128]{2,1,0:T(8,128)(2,1)} %bitcast_select_fusion), calls=%async_computation.1 | async-start | bytes 10485760 | tf_op jit(solution)/shard_map/all_to_all | solution.py:307
  143.6 3.8 %dynamic-slice_bitcast_fusion = bf16[3,2048,256]{2,1,0:T(8,128)(2,1)} fusion(bf16[2,3,2048,256]{3,2,1,0:T(8,128)(2,1)} %param.35, s32[]{:T(128)S(6)} %select_n.158), kind=kLoop, calls=%fused_computation.14 | loop fusion | bytes 6291460 | tf_op jit(solution)/shard_map/jit(dynamic_index_in_dim)/squeeze | solution.py:279
  148.7 6.1 %pad_maximum_fusion = bf16[32,2,192,256]{3,2,1,0:T(8,128)(2,1)} fusion(bf16[32,1,192,256]{3,2,1,0:T(8,128)(2,1)} %bitcast.34, bf16[32,1,192,256]{3,2,1,0:T(8,128)(2,1)} %bitcast.33), kind=kLoop, calls=%fused_computation.10 | loop fusion | flops 3145728 | bytes 12582912 | tf_op jit(solution)/shard_map/stack | solution.py:336
  154.8 5.2 %gather_fusion.1 = bf16[32,192,256]{2,1,0:T(8,128)(2,1)} fusion(bf16[64,192,256]{2,1,0:T(8,128)(2,1)} %bitcast.109, s32[1024]{0:T(1024)S(1)} %pad_clamp_fusion.1), kind=kCustom, calls=%fused_computation.3 | custom fusion | bytes 6291584 | tf_op jit(solution)/shard_map/jit(_take)/gather | solution.py:341
  160.0 3.9 %broadcast_select_fusion = bf16[32,192,256]{2,1,0:T(8,128)(2,1)} fusion(bf16[32,192,256]{2,1,0:T(8,128)(2,1)} %gather_fusion.1, pred[32]{0:T(512)(128)(4,1)S(1)} %compare_and_fusion.4), kind=kLoop, calls=%fused_computation.15 | loop fusion | flops 1572864 | bytes 6291488 | tf_op jit(solution)/shard_map/jit(_take)/select_n | solution.py:341
  163.9 43.6 %all-to-all-done = bf16[128,160,128]{2,1,0:T(8,128)(2,1)} async-done(((bf16[128,160,128]{2,1,0:T(8,128)(2,1)}), bf16[128,160,128]{2,1,0:T(8,128)(2,1)}, u32[]{:S(2)}, u32[]{:S(2)}) %all-to-all-start) | async-done | bytes 5242912 | tf_op jit(solution)/shard_map/all_to_all | solution.py:307
  207.5 4.8 %all-to-all-start.4 = ((bf16[32,192,256]{2,1,0:T(8,128)(2,1)}), bf16[32,192,256]{2,1,0:T(8,128)(2,1)}, u32[]{:S(2)}, u32[]{:S(2)}) async-start(bf16[32,192,256]{2,1,0:T(8,128)(2,1)} %broadcast_select_fusion), calls=%async_computation.5 | async-start | bytes 6291456 | tf_op jit(solution)/shard_map/all_to_all | solution.py:342
  212.4 8.8 %reshape.287 = bf16[1280,2048]{1,0:T(8,128)(2,1)} reshape(bf16[128,160,128]{2,1,0:T(8,128)(2,1)} %all-to-all-done) | data formatting | bytes 10485760 | tf_op jit(solution)/shard_map/reshape | solution.py:289
  221.2 5.5 %fusion.7 = f32[1280,256]{1,0:T(8,128)} fusion(bf16[1280,2048]{1,0:T(8,128)(2,1)} %reshape.287, bf16[2,3,2048,256]{3,2,1,0:T(8,128)(2,1)} %param.35, s32[]{:T(128)S(6)} %select_n.157), kind=kOutput, calls=%fused_computation.33 | convolution fusion | flops 1342177280 | bytes 7602180 | tf_op jit(solution)/shard_map/dot_general | solution.py:311
  229.5 11.2 %convolution_convert_fusion.1 = bf16[1280,2048]{1,0:T(8,128)(2,1)} fusion(bf16[1280,2048]{1,0:T(8,128)(2,1)} %reshape.287, f32[1280,256]{1,0:T(8,128)} %fusion.7, bf16[2,3,2048,256]{3,2,1,0:T(8,128)(2,1)} %param.35, s32[]{:T(128)S(6)} %select_n.157, s32[]{:T(128)S(6)} %add.207, s32[]{:T(128)S(6)} %add.206), kind=kOutput, calls=%fused_computation.9 | convolution fusion | flops 2688942080 | bytes 13895680 | tf_op jit(solution)/shard_map/dot_general | solution.py:314
  240.7 12.4 %add_convert_fusion = bf16[1280,2048]{1,0:T(8,128)(2,1)} fusion(bf16[1280,2048]{1,0:T(8,128)(2,1)} %convolution_convert_fusion.1, bf16[3,2048,256]{2,1,0:T(8,128)(2,1)} %collective-permute-done, f32[1280,256]{1,0:T(8,128)S(1)} %fusion.6, bf16[1280,2048]{1,0:T(8,128)(2,1)} %reshape.287), kind=kOutput, calls=%fused_computation.7 | convolution fusion | flops 2699427840 | bytes 19136512 | tf_op jit(solution)/shard_map/dot_general | solution.py:314
  253.1 8.9 %reshape.288 = bf16[128,160,128]{2,1,0:T(8,128)(2,1)} reshape(bf16[1280,2048]{1,0:T(8,128)(2,1)} %add_convert_fusion) | data formatting | bytes 10485760 | tf_op jit(solution)/shard_map/reshape | solution.py:286
  262.1 8.7 %all-to-all-start.3 = ((bf16[128,160,128]{2,1,0:T(8,128)(2,1)}), bf16[128,160,128]{2,1,0:T(8,128)(2,1)}, u32[]{:S(2)}, u32[]{:S(2)}) async-start(bf16[128,160,128]{2,1,0:T(8,128)(2,1)} %reshape.288), calls=%async_computation.4 | async-start | bytes 10485760 | tf_op jit(solution)/shard_map/all_to_all | solution.py:319
  270.9 63.8 %all-to-all-done.3 = bf16[128,160,128]{2,1,0:T(8,128)(2,1)} async-done(((bf16[128,160,128]{2,1,0:T(8,128)(2,1)}), bf16[128,160,128]{2,1,0:T(8,128)(2,1)}, u32[]{:S(2)}, u32[]{:S(2)}) %all-to-all-start.3) | async-done | bytes 5242912 | tf_op jit(solution)/shard_map/all_to_all | solution.py:319
  338.4 4.9 %gather_fusion.2 = bf16[512,16,128]{2,1,0:T(8,128)(2,1)} fusion(bf16[1280,16,128]{2,1,0:T(8,128)(2,1)} %bitcast.31, s32[1024]{0:T(1024)S(1)} %get-tuple-element.53), kind=kCustom, calls=%fused_computation.clone | custom fusion | bytes 4196352 | tf_op jit(solution)/shard_map/jit(_take)/gather | solution.py:327
  343.2 5.5 %multiply_reduce_fusion = f32[64,16,128]{2,1,0:T(8,128)S(1)} fusion(f32[64,8]{1,0:T(8,128)S(1)} %copy.56, bf16[512,16,128]{2,1,0:T(8,128)(2,1)S(1)} %gather_fusion.3, pred[512]{0:T(512)(128)(4,1)S(1)} %get-tuple-element.42, bf16[512,16,128]{2,1,0:T(8,128)(2,1)} %gather_fusion.2, pred[512]{0:T(512)(128)(4,1)S(1)} %get-tuple-element.26), kind=kLoop, calls=%fused_computation.12 | loop fusion | flops 7208960 | bytes 4721664 | tf_op jit(solution)/shard_map/reduce_sum | solution.py:329
  (122 shorter events, 51.4 us)
Async XLA Ops:
  7.2 47.8 %copy-start = (bf16[512,2048]{1,0:T(8,128)(2,1)S(1)}, bf16[512,2048]{1,0:T(8,128)(2,1)}, u32[]{:S(2)}) copy-start(bf16[512,2048]{1,0:T(8,128)(2,1)} %param.29) | copy-start | bytes 6291460
  35.7 5.6 %copy-start.12 = (s32[1,4]{1,0:T(1,128)S(1)}, s32[1,4]{1,0:T(1,128)}, u32[]{:S(2)}) copy-start(s32[1,4]{1,0:T(1,128)} %param.28) | copy-start | bytes 52
  35.7 6.1 %copy-start.5 = (bf16[32,2,1024]{2,1,0:T(2,128)(2,1)S(1)}, bf16[32,2,1024]{2,1,0:T(2,128)(2,1)}, u32[]{:S(2)}) copy-start(bf16[32,2,1024]{2,1,0:T(2,128)(2,1)} %shard_map.176) | copy-start | bytes 393220
  35.7 7.7 %copy-start.6 = (bf16[256,512]{1,0:T(8,128)(2,1)S(1)}, bf16[256,512]{1,0:T(8,128)(2,1)}, u32[]{:S(2)}) copy-start(bf16[256,512]{1,0:T(8,128)(2,1)} %param.20) | copy-start | bytes 786436
  35.7 8.6 %copy-start.7 = (bf16[256,512]{1,0:T(8,128)(2,1)S(1)}, bf16[256,512]{1,0:T(8,128)(2,1)}, u32[]{:S(2)}) copy-start(bf16[256,512]{1,0:T(8,128)(2,1)} %param.21) | copy-start | bytes 786436
  35.7 9.4 %copy-start.8 = (bf16[256,512]{1,0:T(8,128)(2,1)S(1)}, bf16[256,512]{1,0:T(8,128)(2,1)}, u32[]{:S(2)}) copy-start(bf16[256,512]{1,0:T(8,128)(2,1)} %param.22) | copy-start | bytes 786436
  35.7 43.5 %all-to-all-start.1 = ((bf16[32,192,256]{2,1,0:T(8,128)(2,1)}), bf16[32,192,256]{2,1,0:T(8,128)(2,1)}, u32[]{:S(2)}, u32[]{:S(2)}) async-start(bf16[32,192,256]{2,1,0:T(8,128)(2,1)} %bitcast.110), calls=%async_computation.2 | async-start | bytes 6291456 | tf_op jit(solution)/shard_map/all_to_all | solution.py:267
  40.7 62.5 %reduce-scatter.2.cloned.1.call-start = ((), (), s32[]{:S(2)}) async-start(), calls=%async_computation.6 | async-start | bytes 2621440 | tf_op jit(solution)/shard_map/reduce_scatter | solution.py:233
  83.0 5.2 %copy-start.10 = (s32[64,8]{0,1:T(8,128)S(1)}, s32[64,8]{0,1:T(8,128)}, u32[]{:S(2)}) copy-start(s32[64,8]{0,1:T(8,128)} %param.31) | copy-start | bytes 6148
  83.0 6.9 %copy-start.13 = (s32[64]{0:T(128)S(1)}, s32[64]{0:T(128)}, u32[]{:S(2)}) copy-start(s32[64]{0:T(128)} %param.33) | copy-start | bytes 772
  83.0 20.2 %copy-start.4 = (bf16[64,2048]{1,0:T(8,128)(2,1)S(1)}, bf16[64,2048]{1,0:T(8,128)(2,1)}, u32[]{:S(2)}) copy-start(bf16[64,2048]{1,0:T(8,128)(2,1)} %param.19) | copy-start | bytes 786436
  83.0 21.4 %copy-start.9 = (f32[2048]{0:T(1024)S(1)}, f32[2048]{0:T(1024)}, u32[]{:S(2)}) copy-start(f32[2048]{0:T(1024)} %param.30) | copy-start | bytes 24580
  83.0 51.8 %all-to-all-start.2 = ((bf16[32,192,256]{2,1,0:T(8,128)(2,1)}), bf16[32,192,256]{2,1,0:T(8,128)(2,1)}, u32[]{:S(2)}, u32[]{:S(2)}) async-start(bf16[32,192,256]{2,1,0:T(8,128)(2,1)} %bitcast.111), calls=%async_computation.3 | async-start | bytes 6291456 | tf_op jit(solution)/shard_map/all_to_all | solution.py:267
  134.8 72.7 %all-to-all-start = ((bf16[128,160,128]{2,1,0:T(8,128)(2,1)}), bf16[128,160,128]{2,1,0:T(8,128)(2,1)}, u32[]{:S(2)}, u32[]{:S(2)}) async-start(bf16[128,160,128]{2,1,0:T(8,128)(2,1)} %bitcast_select_fusion), calls=%async_computation.1 | async-start | bytes 10485760 | tf_op jit(solution)/shard_map/all_to_all | solution.py:307
  143.6 4.9 %copy-start.14 = (s32[32]{0:T(128)S(1)}, s32[32]{0:T(128)}, u32[]{:S(2)}) copy-start(s32[32]{0:T(128)} %param.34) | copy-start | bytes 388
  147.4 79.3 %collective-permute-start = (bf16[3,2048,256]{2,1,0:T(8,128)(2,1)}, bf16[3,2048,256]{2,1,0:T(8,128)(2,1)}, u32[]{:S(2)}, u32[]{:S(2)}) collective-permute-start(bf16[3,2048,256]{2,1,0:T(8,128)(2,1)} %dynamic-slice_bitcast_fusion), channel_id=1, source_target_pairs={{0,1},{1,0},{2,3},{3,2},{4,5},{5,4},{6,7},{7,6},{8,9},{9,8},{10,11... | collective-permute-start | bytes 9437192 | tf_op jit(solution)/shard_map/ppermute | solution.py:281
  207.5 54.5 %all-to-all-start.4 = ((bf16[32,192,256]{2,1,0:T(8,128)(2,1)}), bf16[32,192,256]{2,1,0:T(8,128)(2,1)}, u32[]{:S(2)}, u32[]{:S(2)}) async-start(bf16[32,192,256]{2,1,0:T(8,128)(2,1)} %broadcast_select_fusion), calls=%async_computation.5 | async-start | bytes 6291456 | tf_op jit(solution)/shard_map/all_to_all | solution.py:342
  221.2 5.5 %copy-start.2 = (bf16[1280,2048]{1,0:T(8,128)(2,1)S(1)}, bf16[1280,2048]{1,0:T(8,128)(2,1)}, u32[]{:S(2)}) copy-start(bf16[1280,2048]{1,0:T(8,128)(2,1)} %reshape.287) | copy-start | bytes 15728644
  262.0 8.7 %copy-start.11 = (f32[64,8]{0,1:T(8,128)S(1)}, f32[64,8]{0,1:T(8,128)}, u32[]{:S(2)}) copy-start(f32[64,8]{0,1:T(8,128)} %param.32) | copy-start | bytes 6148
  262.1 72.7 %all-to-all-start.3 = ((bf16[128,160,128]{2,1,0:T(8,128)(2,1)}), bf16[128,160,128]{2,1,0:T(8,128)(2,1)}, u32[]{:S(2)}, u32[]{:S(2)}) async-start(bf16[128,160,128]{2,1,0:T(8,128)(2,1)} %reshape.288), calls=%async_computation.4 | async-start | bytes 10485760 | tf_op jit(solution)/shard_map/all_to_all | solution.py:319
  343.2 5.6 %copy-start.3 = (f32[64,2048]{1,0:T(8,128)S(1)}, f32[64,2048]{1,0:T(8,128)}, u32[]{:S(2)}) copy-start(f32[64,2048]{1,0:T(8,128)} %reduce-scatter.2.cloned.1.call-done) | copy-start | bytes 1572868
  348.8 4.7 %copy-start.1 = (bf16[512,2048]{1,0:T(8,128)(2,1)S(1)}, bf16[512,2048]{1,0:T(8,128)(2,1)}, u32[]{:S(2)}) copy-start(bf16[512,2048]{1,0:T(8,128)(2,1)} %param.29) | copy-start | bytes 6291460
Sparse Core Ops, SparseCore 0:
  57.2 45.9 reduce-scatter.1

commit v5 on v2

--- a/solution.py
+++ b/solution.py
@@ -14,15 +14,6 @@
 def cache_kernel(n, need_ref, both_ref, out_ref, stage, send_buf, land, sems):
     me = lax.axis_index("req")
     ex = lax.axis_index("exp")
-    barrier = pltpu.get_barrier_semaphore()
-
-    def greet(k, carry):
-        peer = lax.rem(me + k, n)
-        pl.semaphore_signal(barrier, inc=1, device_id=(peer, ex), device_id_type=MESH)
-        return carry
-
-    lax.fori_loop(1, n, greet, 0)
-    pl.semaphore_wait(barrier, n - 1)
 
     def first_copy(k, peer):
         return pltpu.make_async_remote_copy(
@@ -118,7 +109,7 @@
             pltpu.VMEM(shape, both_t.dtype),
             pltpu.SemaphoreType.DMA((4, n)),
         ],
-        compiler_params=pltpu.CompilerParams(collective_id=0, has_side_effects=True),
+        compiler_params=pltpu.CompilerParams(has_side_effects=True),
     )(need_flat, both_t)
 
 

time: 363 us -> 370 us (1.019)
  Pallas kernels: 20.2 us -> 25.3 us
    pallas_call x1, Pallas kernels: 20.2 us -> 25.3 us  [exchange_cache(): pl.pallas_call(functools.partial(cache_kernel, n), out_shape=jax.ShapeDty...]
  transfers between devices with their start and end apart: 7 -> 7, of which waited for: 5 -> 5; matrix products, arithmetic and copies ran while one was open for 30% -> 29% of each run, Pallas kernels for 0% -> 0%
where the time goes in v5:
time: 370 us; the launch traced here: 368 us
  waiting for transfers between devices  159 us (43%)
  local copies, waits for them, and re-layouts  60.4 us (16%)
  other arithmetic  38 us (10%)
  matrix products  38 us (10%)
  starting transfers between devices  32.9 us (9%)
  Pallas kernels  25.3 us (7%)
  between operations  14.6 us (4%)
    all_to_all x1, waiting for transfers between devices, body(): lax.all_to_all(partial_value, ('req', 'exp'), split_axis=0, concat_axis=0...  63.8 us
    all_to_all x1, waiting for transfers between devices, body(): lax.all_to_all(copies, ('req', 'exp'), split_axis=0, concat_axis=0, tiled...  47.3 us
    all_to_all x2, waiting for transfers between devices, body(): lax.all_to_all(slot_weights[c].reshape(req_count, piece_rows, slot_weight...  33.2 us
    pallas_call x1, Pallas kernels, exchange_cache(): pl.pallas_call(functools.partial(cache_kernel, n), out_shape=jax.ShapeDty...  25.3 us
    dot_general x2, matrix products, body(): lax.dot_general(hidden, part[2], (((1,), (1,)), ((), ())), preferred_elem...  23.6 us
    reduce_scatter x1, waiting for transfers between devices, body(): lax.psum_scatter(jnp.dot(attended, out_proj, preferred_element_type=jnp.f...  14.3 us
    all_to_all x2, starting transfers between devices, body(): lax.all_to_all(slot_weights[c].reshape(req_count, piece_rows, slot_weight...  11.4 us
    select_n x1, other arithmetic, body(): jnp.where(copy_filled[..., None, None], normed_tiles[copy_token], jnp.bfl...  9.43 us
  transfers between devices with their start and end apart: 7, of which 5 were waited for; matrix products, arithmetic and copies ran while one was open for 29% of the time, Pallas kernels for 0%

profile of v5, /device:TPU:1, one launch (start us, length us, event | category | flops | bytes accessed | tf_op | source)
XLA Modules:
  0.0 367.8 jit_solution(18242996239486663859)
XLA Ops:
  11.8 25.3 %shard_map.176 = bf16[32,2,1024]{2,1,0:T(2,128)(2,1)} custom-call(s32[64]{0:T(128)} %reshape.278.need_ref, bf16[32,2,1024]{2,1,0:T(2,128)(2,1)} %maximum_bitcast_fusion.both_ref), custom_call_target="tpu_custom_call" | custom-call | tf_op jit(solution)/shard_map/pallas_call | solution.py:98
  37.1 6.5 %fusion.63 = (bf16[1,3,2048,256]{3,2,1,0:T(8,128)(2,1)}, bf16[1,3,2048,256]{3,2,1,0:T(8,128)(2,1)}, bf16[3,2048,256]{2,1,0:T(8,128)(2,1)}) fusion(bf16[2,3,2048,256]{3,2,1,0:T(8,128)(2,1)} %param.35, s32[]{:T(128)S(6)} %select_n.158), kind=kLoop, calls=%fused_computation.156 | loop fusion | bytes 18874372 | tf_op jit(solution)/shard_map/slice | solution.py:315
  43.6 6.1 %all-to-all-start.2 = ((bf16[32,192,256]{2,1,0:T(8,128)(2,1)}), bf16[32,192,256]{2,1,0:T(8,128)(2,1)}, u32[]{:S(2)}, u32[]{:S(2)}) async-start(bf16[32,192,256]{2,1,0:T(8,128)(2,1)} %bitcast.109), calls=%async_computation.3 | async-start | bytes 6291456 | tf_op jit(solution)/shard_map/all_to_all | solution.py:314
  66.4 21.9 %all-to-all-done.2 = bf16[32,192,256]{2,1,0:T(8,128)(2,1)} async-done(((bf16[32,192,256]{2,1,0:T(8,128)(2,1)}), bf16[32,192,256]{2,1,0:T(8,128)(2,1)}, u32[]{:S(2)}, u32[]{:S(2)}) %all-to-all-start.2) | async-done | bytes 3145760 | tf_op jit(solution)/shard_map/all_to_all | solution.py:314
  88.4 5.4 %all-to-all-start.3 = ((bf16[32,192,256]{2,1,0:T(8,128)(2,1)}), bf16[32,192,256]{2,1,0:T(8,128)(2,1)}, u32[]{:S(2)}, u32[]{:S(2)}) async-start(bf16[32,192,256]{2,1,0:T(8,128)(2,1)} %bitcast.108), calls=%async_computation.4 | async-start | bytes 6291456 | tf_op jit(solution)/shard_map/all_to_all | solution.py:314
  101.9 14.3 %reduce-scatter.2.cloned.1.call-done = f32[64,2048]{1,0:T(8,128)} async-done(((f32[256,2048]{1,0:T(8,128)}), f32[64,2048]{1,0:T(8,128)}) %reduce-scatter.2.cloned.1.call-update) | async-done | bytes 524304 | tf_op jit(solution)/shard_map/reduce_scatter | solution.py:224
  118.6 5.0 %gather_fusion = bf16[1280,16,128]{2,1,0:T(8,128)(2,1)} fusion(bf16[64,16,128]{2,1,0:T(8,128)(2,1)S(1)} %bitcast.105, s32[2048]{0:T(1024)S(1)} %pad_clamp_fusion), kind=kCustom, calls=%fused_computation.2 | custom fusion | bytes 10490880 | tf_op jit(solution)/shard_map/gather | solution.py:279
  123.6 9.4 %bitcast_select_fusion = bf16[128,160,128]{2,1,0:T(8,128)(2,1)} fusion(pred[128,160]{1,0:T(8,128)(4,1)S(1)} %broadcast_in_dim.210, bf16[128,160,128]{2,1,0:T(8,128)(2,1)} %bitcast.106), kind=kLoop, calls=%fused_computation.11 | loop fusion | flops 2621440 | bytes 10506240 | tf_op jit(solution)/shard_map/jit(_where)/select_n | solution.py:278
  133.1 11.3 %all-to-all-done.3 = bf16[32,192,256]{2,1,0:T(8,128)(2,1)} async-done(((bf16[32,192,256]{2,1,0:T(8,128)(2,1)}), bf16[32,192,256]{2,1,0:T(8,128)(2,1)}, u32[]{:S(2)}, u32[]{:S(2)}) %all-to-all-start.3) | async-done | bytes 3145760 | tf_op jit(solution)/shard_map/all_to_all | solution.py:314
  144.3 6.5 %all-to-all-start = ((bf16[128,160,128]{2,1,0:T(8,128)(2,1)}), bf16[128,160,128]{2,1,0:T(8,128)(2,1)}, u32[]{:S(2)}, u32[]{:S(2)}) async-start(bf16[128,160,128]{2,1,0:T(8,128)(2,1)} %bitcast_select_fusion), calls=%async_computation.1 | async-start | bytes 10485760 | tf_op jit(solution)/shard_map/all_to_all | solution.py:282
  152.5 6.1 %pad_maximum_fusion = bf16[32,2,192,256]{3,2,1,0:T(8,128)(2,1)} fusion(bf16[32,1,192,256]{3,2,1,0:T(8,128)(2,1)} %bitcast.34, bf16[32,1,192,256]{3,2,1,0:T(8,128)(2,1)} %bitcast.32), kind=kLoop, calls=%fused_computation.10 | loop fusion | flops 3145728 | bytes 12582912 | tf_op jit(solution)/shard_map/stack | solution.py:323
  158.6 5.2 %gather_fusion.1 = bf16[32,192,256]{2,1,0:T(8,128)(2,1)} fusion(bf16[64,192,256]{2,1,0:T(8,128)(2,1)} %bitcast.107, s32[1024]{0:T(1024)S(1)} %pad_clamp_fusion.1), kind=kCustom, calls=%fused_computation.3 | custom fusion | bytes 6291584 | tf_op jit(solution)/shard_map/jit(_take)/gather | solution.py:328
  163.8 3.9 %broadcast_select_fusion = bf16[32,192,256]{2,1,0:T(8,128)(2,1)} fusion(bf16[32,192,256]{2,1,0:T(8,128)(2,1)} %gather_fusion.1, pred[32]{0:T(512)(128)(4,1)S(1)} %compare_and_fusion.4), kind=kLoop, calls=%fused_computation.15 | loop fusion | flops 1572864 | bytes 6291488 | tf_op jit(solution)/shard_map/jit(_take)/select_n | solution.py:328
  167.7 47.3 %all-to-all-done = bf16[128,160,128]{2,1,0:T(8,128)(2,1)} async-done(((bf16[128,160,128]{2,1,0:T(8,128)(2,1)}), bf16[128,160,128]{2,1,0:T(8,128)(2,1)}, u32[]{:S(2)}, u32[]{:S(2)}) %all-to-all-start) | async-done | bytes 5242912 | tf_op jit(solution)/shard_map/all_to_all | solution.py:282
  215.0 4.8 %all-to-all-start.4 = ((bf16[32,192,256]{2,1,0:T(8,128)(2,1)}), bf16[32,192,256]{2,1,0:T(8,128)(2,1)}, u32[]{:S(2)}, u32[]{:S(2)}) async-start(bf16[32,192,256]{2,1,0:T(8,128)(2,1)} %broadcast_select_fusion), calls=%async_computation.5 | async-start | bytes 6291456 | tf_op jit(solution)/shard_map/all_to_all | solution.py:329
  219.8 8.8 %reshape.287 = bf16[1280,2048]{1,0:T(8,128)(2,1)} reshape(bf16[128,160,128]{2,1,0:T(8,128)(2,1)} %all-to-all-done) | data formatting | bytes 10485760 | tf_op jit(solution)/shard_map/reshape | solution.py:264
  228.6 5.5 %fusion.7 = f32[1280,256]{1,0:T(8,128)} fusion(bf16[1280,2048]{1,0:T(8,128)(2,1)} %reshape.287, bf16[2,3,2048,256]{3,2,1,0:T(8,128)(2,1)} %param.35, s32[]{:T(128)S(6)} %select_n.157), kind=kOutput, calls=%fused_computation.33 | convolution fusion | flops 1342177280 | bytes 7602180 | tf_op jit(solution)/shard_map/dot_general | solution.py:286
  237.0 11.2 %convolution_convert_fusion.1 = bf16[1280,2048]{1,0:T(8,128)(2,1)} fusion(bf16[1280,2048]{1,0:T(8,128)(2,1)} %reshape.287, f32[1280,256]{1,0:T(8,128)} %fusion.7, bf16[2,3,2048,256]{3,2,1,0:T(8,128)(2,1)} %param.35, s32[]{:T(128)S(6)} %select_n.157, s32[]{:T(128)S(6)} %add.207, s32[]{:T(128)S(6)} %add.206), kind=kOutput, calls=%fused_computation.9 | convolution fusion | flops 2688942080 | bytes 13895680 | tf_op jit(solution)/shard_map/dot_general | solution.py:289
  248.1 12.4 %add_convert_fusion = bf16[1280,2048]{1,0:T(8,128)(2,1)} fusion(bf16[1280,2048]{1,0:T(8,128)(2,1)} %convolution_convert_fusion.1, bf16[3,2048,256]{2,1,0:T(8,128)(2,1)} %collective-permute-done, f32[1280,256]{1,0:T(8,128)S(1)} %fusion.6, bf16[1280,2048]{1,0:T(8,128)(2,1)} %reshape.287), kind=kOutput, calls=%fused_computation.7 | convolution fusion | flops 2699427840 | bytes 19136512 | tf_op jit(solution)/shard_map/dot_general | solution.py:289
  260.5 8.9 %reshape.288 = bf16[128,160,128]{2,1,0:T(8,128)(2,1)} reshape(bf16[1280,2048]{1,0:T(8,128)(2,1)} %add_convert_fusion) | data formatting | bytes 10485760 | tf_op jit(solution)/shard_map/reshape | solution.py:261
  269.5 8.7 %all-to-all-start.1 = ((bf16[128,160,128]{2,1,0:T(8,128)(2,1)}), bf16[128,160,128]{2,1,0:T(8,128)(2,1)}, u32[]{:S(2)}, u32[]{:S(2)}) async-start(bf16[128,160,128]{2,1,0:T(8,128)(2,1)} %reshape.288), calls=%async_computation.2 | async-start | bytes 10485760 | tf_op jit(solution)/shard_map/all_to_all | solution.py:294
  278.3 63.8 %all-to-all-done.1 = bf16[128,160,128]{2,1,0:T(8,128)(2,1)} async-done(((bf16[128,160,128]{2,1,0:T(8,128)(2,1)}), bf16[128,160,128]{2,1,0:T(8,128)(2,1)}, u32[]{:S(2)}, u32[]{:S(2)}) %all-to-all-start.1) | async-done | bytes 5242912 | tf_op jit(solution)/shard_map/all_to_all | solution.py:294
  345.8 4.9 %gather_fusion.3 = bf16[512,16,128]{2,1,0:T(8,128)(2,1)} fusion(bf16[1280,16,128]{2,1,0:T(8,128)(2,1)} %bitcast.29, s32[1024]{0:T(1024)S(1)} %get-tuple-element.45), kind=kCustom, calls=%fused_computation.1.clone | custom fusion | bytes 4196352 | tf_op jit(solution)/shard_map/jit(_take)/gather | solution.py:302
  350.7 5.6 %multiply_reduce_fusion = f32[64,16,128]{2,1,0:T(8,128)S(1)} fusion(f32[64,8]{1,0:T(8,128)S(1)} %copy.56, bf16[512,16,128]{2,1,0:T(8,128)(2,1)} %gather_fusion.3, pred[512]{0:T(512)(128)(4,1)S(1)} %get-tuple-element.35, bf16[512,16,128]{2,1,0:T(8,128)(2,1)S(1)} %gather_fusion.2, pred[512]{0:T(512)(128)(4,1)S(1)} %get-tuple-element.16), kind=kLoop, calls=%fused_computation.12 | loop fusion | flops 7208960 | bytes 4721664 | tf_op jit(solution)/shard_map/reduce_sum | solution.py:304
  (122 shorter events, 44.4 us)
Async XLA Ops:
  7.2 57.2 %copy-start = (bf16[512,2048]{1,0:T(8,128)(2,1)S(1)}, bf16[512,2048]{1,0:T(8,128)(2,1)}, u32[]{:S(2)}) copy-start(bf16[512,2048]{1,0:T(8,128)(2,1)} %param.29) | copy-start | bytes 6291460
  43.6 7.0 %copy-start.13 = (s32[1,4]{1,0:T(1,128)S(1)}, s32[1,4]{1,0:T(1,128)}, u32[]{:S(2)}) copy-start(s32[1,4]{1,0:T(1,128)} %param.28) | copy-start | bytes 52
  43.6 8.6 %copy-start.6 = (bf16[256,512]{1,0:T(8,128)(2,1)S(1)}, bf16[256,512]{1,0:T(8,128)(2,1)}, u32[]{:S(2)}) copy-start(bf16[256,512]{1,0:T(8,128)(2,1)} %param.20) | copy-start | bytes 786436
  43.6 9.0 %copy-start.7 = (bf16[256,512]{1,0:T(8,128)(2,1)S(1)}, bf16[256,512]{1,0:T(8,128)(2,1)}, u32[]{:S(2)}) copy-start(bf16[256,512]{1,0:T(8,128)(2,1)} %param.21) | copy-start | bytes 786436
  43.6 44.8 %all-to-all-start.2 = ((bf16[32,192,256]{2,1,0:T(8,128)(2,1)}), bf16[32,192,256]{2,1,0:T(8,128)(2,1)}, u32[]{:S(2)}, u32[]{:S(2)}) async-start(bf16[32,192,256]{2,1,0:T(8,128)(2,1)} %bitcast.109), calls=%async_computation.3 | async-start | bytes 6291456 | tf_op jit(solution)/shard_map/all_to_all | solution.py:314
  49.7 4.5 %copy-start.5 = (bf16[32,2,1024]{2,1,0:T(2,128)(2,1)S(1)}, bf16[32,2,1024]{2,1,0:T(2,128)(2,1)}, u32[]{:S(2)}) copy-start(bf16[32,2,1024]{2,1,0:T(2,128)(2,1)} %shard_map.176) | copy-start | bytes 393220
  49.7 66.5 %reduce-scatter.2.cloned.1.call-start = ((), (), s32[]{:S(2)}) async-start(), calls=%async_computation.6 | async-start | bytes 2621440 | tf_op jit(solution)/shard_map/reduce_scatter | solution.py:224
  56.1 4.2 %copy-start.9 = (pred[256,320]{0,1:T(8,128)(4,1)S(1)}, pred[256,320]{0,1:T(8,128)(4,1)}, u32[]{:S(2)}) copy-start(pred[256,320]{0,1:T(8,128)(4,1)} %broadcast_compare_fusion) | copy-start | bytes 245764
  59.8 2.8 copy-start.8
  88.4 5.4 %copy-start.11 = (s32[64,8]{0,1:T(8,128)S(1)}, s32[64,8]{0,1:T(8,128)}, u32[]{:S(2)}) copy-start(s32[64,8]{0,1:T(8,128)} %param.31) | copy-start | bytes 6148
  88.4 7.2 %copy-start.14 = (s32[64]{0:T(128)S(1)}, s32[64]{0:T(128)}, u32[]{:S(2)}) copy-start(s32[64]{0:T(128)} %param.33) | copy-start | bytes 772
  88.4 27.8 %copy-start.4 = (bf16[64,2048]{1,0:T(8,128)(2,1)S(1)}, bf16[64,2048]{1,0:T(8,128)(2,1)}, u32[]{:S(2)}) copy-start(bf16[64,2048]{1,0:T(8,128)(2,1)} %param.19) | copy-start | bytes 786436
  88.4 29.0 %copy-start.10 = (f32[2048]{0:T(1024)S(1)}, f32[2048]{0:T(1024)}, u32[]{:S(2)}) copy-start(f32[2048]{0:T(1024)} %param.30) | copy-start | bytes 24580
  88.4 56.0 %all-to-all-start.3 = ((bf16[32,192,256]{2,1,0:T(8,128)(2,1)}), bf16[32,192,256]{2,1,0:T(8,128)(2,1)}, u32[]{:S(2)}, u32[]{:S(2)}) async-start(bf16[32,192,256]{2,1,0:T(8,128)(2,1)} %bitcast.108), calls=%async_computation.4 | async-start | bytes 6291456 | tf_op jit(solution)/shard_map/all_to_all | solution.py:314
  133.1 19.2 %copy-start.15 = (s32[32]{0:T(128)S(1)}, s32[32]{0:T(128)}, u32[]{:S(2)}) copy-start(s32[32]{0:T(128)} %param.34) | copy-start | bytes 388
  144.3 70.6 %all-to-all-start = ((bf16[128,160,128]{2,1,0:T(8,128)(2,1)}), bf16[128,160,128]{2,1,0:T(8,128)(2,1)}, u32[]{:S(2)}, u32[]{:S(2)}) async-start(bf16[128,160,128]{2,1,0:T(8,128)(2,1)} %bitcast_select_fusion), calls=%async_computation.1 | async-start | bytes 10485760 | tf_op jit(solution)/shard_map/all_to_all | solution.py:282
  150.9 83.3 %collective-permute-start = (bf16[3,2048,256]{2,1,0:T(8,128)(2,1)}, bf16[3,2048,256]{2,1,0:T(8,128)(2,1)}, u32[]{:S(2)}, u32[]{:S(2)}) collective-permute-start(bf16[3,2048,256]{2,1,0:T(8,128)(2,1)} %get-tuple-element.24), channel_id=1, source_target_pairs={{0,1},{1,0},{2,3},{3,2},{4,5},{5,4},{6,7},{7,6},{8,9},{9,8},{10,11... | collective-permute-start | bytes 9437192 | tf_op jit(solution)/shard_map/ppermute | solution.py:256
  215.0 54.5 %all-to-all-start.4 = ((bf16[32,192,256]{2,1,0:T(8,128)(2,1)}), bf16[32,192,256]{2,1,0:T(8,128)(2,1)}, u32[]{:S(2)}, u32[]{:S(2)}) async-start(bf16[32,192,256]{2,1,0:T(8,128)(2,1)} %broadcast_select_fusion), calls=%async_computation.5 | async-start | bytes 6291456 | tf_op jit(solution)/shard_map/all_to_all | solution.py:329
  228.6 5.5 %copy-start.2 = (bf16[1280,2048]{1,0:T(8,128)(2,1)S(1)}, bf16[1280,2048]{1,0:T(8,128)(2,1)}, u32[]{:S(2)}) copy-start(bf16[1280,2048]{1,0:T(8,128)(2,1)} %reshape.287) | copy-start | bytes 15728644
  269.5 8.7 %copy-start.12 = (f32[64,8]{0,1:T(8,128)S(1)}, f32[64,8]{0,1:T(8,128)}, u32[]{:S(2)}) copy-start(f32[64,8]{0,1:T(8,128)} %param.32) | copy-start | bytes 6148
  269.5 72.7 %all-to-all-start.1 = ((bf16[128,160,128]{2,1,0:T(8,128)(2,1)}), bf16[128,160,128]{2,1,0:T(8,128)(2,1)}, u32[]{:S(2)}, u32[]{:S(2)}) async-start(bf16[128,160,128]{2,1,0:T(8,128)(2,1)} %reshape.288), calls=%async_computation.2 | async-start | bytes 10485760 | tf_op jit(solution)/shard_map/all_to_all | solution.py:294
  350.7 5.6 %copy-start.3 = (f32[64,2048]{1,0:T(8,128)S(1)}, f32[64,2048]{1,0:T(8,128)}, u32[]{:S(2)}) copy-start(f32[64,2048]{1,0:T(8,128)} %reduce-scatter.2.cloned.1.call-done) | copy-start | bytes 1572868
  356.3 4.7 %copy-start.1 = (bf16[512,2048]{1,0:T(8,128)(2,1)S(1)}, bf16[512,2048]{1,0:T(8,128)(2,1)}, u32[]{:S(2)}) copy-start(bf16[512,2048]{1,0:T(8,128)(2,1)} %param.29) | copy-start | bytes 6291460
Sparse Core Ops, SparseCore 0:
  66.6 49.5 reduce-scatter.1

commit v6 on v2

--- a/solution.py
+++ b/solution.py
@@ -289,11 +289,18 @@
     )
     copies = copies.reshape(req_count * exp_count, tile_rows, lanes)
     inbox = lax.all_to_all(copies, ("req", "exp"), split_axis=0, concat_axis=0, tiled=True)
-    in_rows = as_rows(inbox)
+    in_rows = inbox.reshape(req_count * exp_count * capacity, tile_high, lanes)
+    tiled_dims = (((1, 2), (0, 1)), ((), ()))
     halves = []
     for part in (own_part, got_part):
-        gate_act = jnp.dot(in_rows, part[0], preferred_element_type=jnp.float32)
-        up_act = jnp.dot(in_rows, part[1], preferred_element_type=jnp.float32)
+        gate_act = lax.dot_general(
+            in_rows, part[0].reshape(tile_high, lanes, -1), tiled_dims,
+            preferred_element_type=jnp.float32,
+        )
+        up_act = lax.dot_general(
+            in_rows, part[1].reshape(tile_high, lanes, -1), tiled_dims,
+            preferred_element_type=jnp.float32,
+        )
         hidden = (jax.nn.silu(gate_act) * up_act).astype(jnp.bfloat16)
         piece = lax.dot_general(
             hidden, part[2], (((1,), (1,)), ((), ())), preferred_element_type=jnp.float32

time: 363 us -> 355 us (0.978)
  local copies, waits for them, and re-layouts: 60.4 us -> 56.5 us
    reshape x1 -> x0, local copies, waits for them, and re-layouts: 8.82 us -> none  [as_rows(): return tiles.reshape(req_count * exp_count * capacity, model_width)]
    all_to_all x1, waiting for transfers between devices: 47.3 us -> 42.9 us  [body(): lax.all_to_all(copies, ('req', 'exp'), split_axis=0, concat_axis=0, tiled...]
    slice x1 -> x3, local copies, waits for them, and re-layouts: 0.23 us -> 4.57 us  [the longest x1 2.66 us: body(): part[1].reshape(tile_high, lanes, -1)]
    dot_general x2, matrix products: 23.6 us -> 19.7 us  [body(): lax.dot_general(hidden, part[2], (((1,), (1,)), ((), ())), preferred_elem...]
  transfers between devices with their start and end apart: 7 -> 7, of which waited for: 5 -> 6; matrix products, arithmetic and copies ran while one was open for 30% -> 29% of each run, Pallas kernels for 0% -> 0%
where the time goes in v6:
time: 355 us; the launch traced here: 354 us
  waiting for transfers between devices  155 us (44%)
  local copies, waits for them, and re-layouts  56.5 us (16%)
  other arithmetic  38.6 us (11%)
  matrix products  36.1 us (10%)
  starting transfers between devices  32.4 us (9%)
  Pallas kernels  20.2 us (6%)
  between operations  14.6 us (4%)
    all_to_all x1, waiting for transfers between devices, body(): lax.all_to_all(partial_value, ('req', 'exp'), split_axis=0, concat_axis=0...  63.8 us
    all_to_all x1, waiting for transfers between devices, body(): lax.all_to_all(copies, ('req', 'exp'), split_axis=0, concat_axis=0, tiled...  42.9 us
    all_to_all x2, waiting for transfers between devices, body(): lax.all_to_all(slot_weights[c].reshape(req_count, piece_rows, slot_weight...  28.4 us
    pallas_call x1, Pallas kernels, exchange_cache(): pl.pallas_call(functools.partial(cache_kernel, n), out_shape=jax.ShapeDty...  20.2 us
    dot_general x2, matrix products, body(): lax.dot_general(hidden, part[2], (((1,), (1,)), ((), ())), preferred_elem...  19.7 us
    reduce_scatter x1, waiting for transfers between devices, body(): lax.psum_scatter(jnp.dot(attended, out_proj, preferred_element_type=jnp.f...  17.9 us
    dot_general x2, matrix products, body(): lax.dot_general(in_rows, part[0].reshape(tile_high, lanes, -1), tiled_dim...  10.3 us
    all_to_all x2, starting transfers between devices, body(): lax.all_to_all(slot_weights[c].reshape(req_count, piece_rows, slot_weight...  10.1 us
  transfers between devices with their start and end apart: 7, of which 6 were waited for; matrix products, arithmetic and copies ran while one was open for 29% of the time, Pallas kernels for 0%

profile of v6, /device:TPU:1, one launch (start us, length us, event | category | flops | bytes accessed | tf_op | source)
XLA Modules:
  0.0 353.8 jit_solution(406017147272859646)
XLA Ops:
  11.8 20.2 %shard_map.176 = bf16[32,2,1024]{2,1,0:T(2,128)(2,1)} custom-call(s32[64]{0:T(128)} %reshape.278.need_ref, bf16[32,2,1024]{2,1,0:T(2,128)(2,1)} %maximum_bitcast_fusion.both_ref), custom_call_target="tpu_custom_call" | custom-call | tf_op jit(solution)/shard_map/pallas_call | solution.py:107
  32.0 6.5 %fusion.94 = (bf16[1,3,2048,256]{3,2,1,0:T(8,128)(2,1)}, bf16[1,3,2048,256]{3,2,1,0:T(8,128)(2,1)}, bf16[3,2048,256]{2,1,0:T(8,128)(2,1)}) fusion(bf16[2,3,2048,256]{3,2,1,0:T(8,128)(2,1)} %param.35, s32[]{:T(128)S(6)} %select_n.158), kind=kLoop, calls=%fused_computation.167 | loop fusion | bytes 18874372 | tf_op jit(solution)/shard_map/slice | solution.py:331
  38.5 5.0 %all-to-all-start.3 = ((bf16[32,192,256]{2,1,0:T(8,128)(2,1)}), bf16[32,192,256]{2,1,0:T(8,128)(2,1)}, u32[]{:S(2)}, u32[]{:S(2)}) async-start(bf16[32,192,256]{2,1,0:T(8,128)(2,1)} %bitcast.115), calls=%async_computation.4 | async-start | bytes 6291456 | tf_op jit(solution)/shard_map/all_to_all | solution.py:330
  61.4 20.6 %all-to-all-done.3 = bf16[32,192,256]{2,1,0:T(8,128)(2,1)} async-done(((bf16[32,192,256]{2,1,0:T(8,128)(2,1)}), bf16[32,192,256]{2,1,0:T(8,128)(2,1)}, u32[]{:S(2)}, u32[]{:S(2)}) %all-to-all-start.3) | async-done | bytes 3145760 | tf_op jit(solution)/shard_map/all_to_all | solution.py:330
  82.0 5.1 %all-to-all-start.2 = ((bf16[32,192,256]{2,1,0:T(8,128)(2,1)}), bf16[32,192,256]{2,1,0:T(8,128)(2,1)}, u32[]{:S(2)}, u32[]{:S(2)}) async-start(bf16[32,192,256]{2,1,0:T(8,128)(2,1)} %bitcast.114), calls=%async_computation.3 | async-start | bytes 6291456 | tf_op jit(solution)/shard_map/all_to_all | solution.py:330
  95.3 17.9 %reduce-scatter.2.cloned.1.call-done = f32[64,2048]{1,0:T(8,128)} async-done(((f32[256,2048]{1,0:T(8,128)}), f32[64,2048]{1,0:T(8,128)}) %reduce-scatter.2.cloned.1.call-update) | async-done | bytes 524304 | tf_op jit(solution)/shard_map/reduce_scatter | solution.py:233
  115.6 5.0 %gather_fusion = bf16[1280,16,128]{2,1,0:T(8,128)(2,1)} fusion(bf16[64,16,128]{2,1,0:T(8,128)(2,1)S(1)} %bitcast.111, s32[2048]{0:T(1024)S(1)} %pad_clamp_fusion), kind=kCustom, calls=%fused_computation.2 | custom fusion | bytes 10490880 | tf_op jit(solution)/shard_map/gather | solution.py:288
  120.6 9.4 %bitcast_select_fusion = bf16[128,160,128]{2,1,0:T(8,128)(2,1)} fusion(pred[128,160]{1,0:T(8,128)(4,1)S(1)} %broadcast_in_dim.210, bf16[128,160,128]{2,1,0:T(8,128)(2,1)} %bitcast.112), kind=kLoop, calls=%fused_computation.11 | loop fusion | flops 2621440 | bytes 10506240 | tf_op jit(solution)/shard_map/jit(_where)/select_n | solution.py:287
  130.1 7.8 %all-to-all-done.2 = bf16[32,192,256]{2,1,0:T(8,128)(2,1)} async-done(((bf16[32,192,256]{2,1,0:T(8,128)(2,1)}), bf16[32,192,256]{2,1,0:T(8,128)(2,1)}, u32[]{:S(2)}, u32[]{:S(2)}) %all-to-all-start.2) | async-done | bytes 3145760 | tf_op jit(solution)/shard_map/all_to_all | solution.py:330
  137.8 7.3 %all-to-all-start = ((bf16[128,160,128]{2,1,0:T(8,128)(2,1)}), bf16[128,160,128]{2,1,0:T(8,128)(2,1)}, u32[]{:S(2)}, u32[]{:S(2)}) async-start(bf16[128,160,128]{2,1,0:T(8,128)(2,1)} %bitcast_select_fusion), calls=%async_computation.1 | async-start | bytes 10485760 | tf_op jit(solution)/shard_map/all_to_all | solution.py:291
  148.3 6.1 %pad_maximum_fusion = bf16[32,2,192,256]{3,2,1,0:T(8,128)(2,1)} fusion(bf16[32,1,192,256]{3,2,1,0:T(8,128)(2,1)} %bitcast.39, bf16[32,1,192,256]{3,2,1,0:T(8,128)(2,1)} %bitcast.37), kind=kLoop, calls=%fused_computation.10 | loop fusion | flops 3145728 | bytes 12582912 | tf_op jit(solution)/shard_map/stack | solution.py:339
  154.4 5.2 %gather_fusion.1 = bf16[32,192,256]{2,1,0:T(8,128)(2,1)} fusion(bf16[64,192,256]{2,1,0:T(8,128)(2,1)} %bitcast.113, s32[1024]{0:T(1024)S(1)} %pad_clamp_fusion.1), kind=kCustom, calls=%fused_computation.3 | custom fusion | bytes 6291584 | tf_op jit(solution)/shard_map/jit(_take)/gather | solution.py:344
  159.6 3.9 %broadcast_select_fusion = bf16[32,192,256]{2,1,0:T(8,128)(2,1)} fusion(bf16[32,192,256]{2,1,0:T(8,128)(2,1)} %gather_fusion.1, pred[32]{0:T(512)(128)(4,1)S(1)} %compare_and_fusion.4), kind=kLoop, calls=%fused_computation.23 | loop fusion | flops 1572864 | bytes 6291488 | tf_op jit(solution)/shard_map/jit(_take)/select_n | solution.py:344
  166.2 42.9 %all-to-all-done = bf16[128,160,128]{2,1,0:T(8,128)(2,1)} async-done(((bf16[128,160,128]{2,1,0:T(8,128)(2,1)}), bf16[128,160,128]{2,1,0:T(8,128)(2,1)}, u32[]{:S(2)}, u32[]{:S(2)}) %all-to-all-start) | async-done | bytes 5242912 | tf_op jit(solution)/shard_map/all_to_all | solution.py:291
  209.1 4.8 %all-to-all-start.4 = ((bf16[32,192,256]{2,1,0:T(8,128)(2,1)}), bf16[32,192,256]{2,1,0:T(8,128)(2,1)}, u32[]{:S(2)}, u32[]{:S(2)}) async-start(bf16[32,192,256]{2,1,0:T(8,128)(2,1)} %broadcast_select_fusion), calls=%async_computation.5 | async-start | bytes 6291456 | tf_op jit(solution)/shard_map/all_to_all | solution.py:345
  214.0 5.2 %fusion.9 = f32[1280,256]{1,0:T(8,128)} fusion(bf16[16,128,256]{2,1,0:T(8,128)(2,1)S(1)} %bitcast.120, bf16[1280,16,128]{2,1,0:T(8,128)(2,1)} %bitcast.22), kind=kOutput, calls=%fused_computation.24 | convolution fusion | flops 1342177280 | bytes 7602176 | tf_op jit(solution)/shard_map/dot_general | solution.py:296
  219.2 5.1 %fusion.18 = f32[1280,256]{1,0:T(8,128)} fusion(bf16[16,128,256]{2,1,0:T(8,128)(2,1)S(1)} %bitcast.123, bf16[1280,16,128]{2,1,0:T(8,128)(2,1)} %bitcast.22), kind=kOutput, calls=%fused_computation.27 | convolution fusion | flops 1342177280 | bytes 7602176 | tf_op jit(solution)/shard_map/dot_general | solution.py:296
  224.3 9.4 %convolution_convert_fusion.1 = bf16[1280,2048]{1,0:T(8,128)(2,1)} fusion(bf16[16,128,256]{2,1,0:T(8,128)(2,1)S(1)} %bitcast.119, bf16[1280,16,128]{2,1,0:T(8,128)(2,1)} %bitcast.22, f32[1280,256]{1,0:T(8,128)} %fusion.9, bf16[2,3,2048,256]{3,2,1,0:T(8,128)(2,1)} %param.35, s32[]{:T(128)S(6)} %select_n.157, s32[]{:T(128)S(6)} %add.207), kind=kOutput, calls=%fused_computation.9 | convolution fusion | flops 2688942080 | bytes 13893640 | tf_op jit(solution)/shard_map/dot_general | solution.py:305
  233.6 10.3 %add_convert_fusion = bf16[1280,2048]{1,0:T(8,128)(2,1)} fusion(bf16[1280,2048]{1,0:T(8,128)(2,1)} %convolution_convert_fusion.1, bf16[3,2048,256]{2,1,0:T(8,128)(2,1)} %collective-permute-done, f32[1280,256]{1,0:T(8,128)} %fusion.18, bf16[16,128,256]{2,1,0:T(8,128)(2,1)S(1)} %bitcast.122, bf16[1280,16,128]{2,1,0:T(8,128)(2,1)} %bitcast.22), kind=kOutput, calls=%fused_computation.7 | convolution fusion | flops 2699427840 | bytes 19136512 | tf_op jit(solution)/shard_map/dot_general | solution.py:305
  244.0 8.9 %reshape.288 = bf16[128,160,128]{2,1,0:T(8,128)(2,1)} reshape(bf16[1280,2048]{1,0:T(8,128)(2,1)} %add_convert_fusion) | data formatting | bytes 10485760 | tf_op jit(solution)/shard_map/reshape | solution.py:270
  255.3 8.9 %all-to-all-start.1 = ((bf16[128,160,128]{2,1,0:T(8,128)(2,1)}), bf16[128,160,128]{2,1,0:T(8,128)(2,1)}, u32[]{:S(2)}, u32[]{:S(2)}) async-start(bf16[128,160,128]{2,1,0:T(8,128)(2,1)} %reshape.288), calls=%async_computation.2 | async-start | bytes 10485760 | tf_op jit(solution)/shard_map/all_to_all | solution.py:310
  264.3 63.8 %all-to-all-done.1 = bf16[128,160,128]{2,1,0:T(8,128)(2,1)} async-done(((bf16[128,160,128]{2,1,0:T(8,128)(2,1)}), bf16[128,160,128]{2,1,0:T(8,128)(2,1)}, u32[]{:S(2)}, u32[]{:S(2)}) %all-to-all-start.1) | async-done | bytes 5242912 | tf_op jit(solution)/shard_map/all_to_all | solution.py:310
  331.8 4.9 %gather_fusion.2 = bf16[512,16,128]{2,1,0:T(8,128)(2,1)} fusion(bf16[1280,16,128]{2,1,0:T(8,128)(2,1)} %bitcast.34, s32[1024]{0:T(1024)S(1)} %get-tuple-element.50), kind=kCustom, calls=%fused_computation.clone | custom fusion | bytes 4196352 | tf_op jit(solution)/shard_map/jit(_take)/gather | solution.py:318
  336.7 5.6 %multiply_reduce_fusion = f32[64,16,128]{2,1,0:T(8,128)S(1)} fusion(f32[64,8]{1,0:T(8,128)S(1)} %copy.62, bf16[512,16,128]{2,1,0:T(8,128)(2,1)S(1)} %gather_fusion.3, pred[512]{0:T(512)(128)(4,1)S(1)} %get-tuple-element.39, bf16[512,16,128]{2,1,0:T(8,128)(2,1)} %gather_fusion.2, pred[512]{0:T(512)(128)(4,1)S(1)} %get-tuple-element.16), kind=kLoop, calls=%fused_computation.12 | loop fusion | flops 7208960 | bytes 4721664 | tf_op jit(solution)/shard_map/reduce_sum | solution.py:320
  (123 shorter events, 49.5 us)
Async XLA Ops:
  7.2 52.1 %copy-start = (bf16[512,2048]{1,0:T(8,128)(2,1)S(1)}, bf16[512,2048]{1,0:T(8,128)(2,1)}, u32[]{:S(2)}) copy-start(bf16[512,2048]{1,0:T(8,128)(2,1)} %param.29) | copy-start | bytes 6291460
  38.4 5.6 %copy-start.13 = (s32[1,4]{1,0:T(1,128)S(1)}, s32[1,4]{1,0:T(1,128)}, u32[]{:S(2)}) copy-start(s32[1,4]{1,0:T(1,128)} %param.28) | copy-start | bytes 52
  38.4 6.9 %copy-start.5 = (bf16[32,2,1024]{2,1,0:T(2,128)(2,1)S(1)}, bf16[32,2,1024]{2,1,0:T(2,128)(2,1)}, u32[]{:S(2)}) copy-start(bf16[32,2,1024]{2,1,0:T(2,128)(2,1)} %shard_map.176) | copy-start | bytes 393220
  38.4 7.7 %copy-start.6 = (bf16[256,512]{1,0:T(8,128)(2,1)S(1)}, bf16[256,512]{1,0:T(8,128)(2,1)}, u32[]{:S(2)}) copy-start(bf16[256,512]{1,0:T(8,128)(2,1)} %param.21) | copy-start | bytes 786436
  38.4 8.6 %copy-start.7 = (bf16[256,512]{1,0:T(8,128)(2,1)S(1)}, bf16[256,512]{1,0:T(8,128)(2,1)}, u32[]{:S(2)}) copy-start(bf16[256,512]{1,0:T(8,128)(2,1)} %param.20) | copy-start | bytes 786436
  38.5 43.5 %all-to-all-start.3 = ((bf16[32,192,256]{2,1,0:T(8,128)(2,1)}), bf16[32,192,256]{2,1,0:T(8,128)(2,1)}, u32[]{:S(2)}, u32[]{:S(2)}) async-start(bf16[32,192,256]{2,1,0:T(8,128)(2,1)} %bitcast.115), calls=%async_computation.4 | async-start | bytes 6291456 | tf_op jit(solution)/shard_map/all_to_all | solution.py:330
  43.4 69.7 %reduce-scatter.2.cloned.1.call-start = ((), (), s32[]{:S(2)}) async-start(), calls=%async_computation.6 | async-start | bytes 2621440 | tf_op jit(solution)/shard_map/reduce_scatter | solution.py:233
  51.0 4.2 %copy-start.9 = (bf16[64,4,128]{2,0,1:T(8,128)(2,1)S(1)}, bf16[64,4,128]{2,0,1:T(8,128)(2,1)}, u32[]{:S(2)}) copy-start(bf16[64,4,128]{2,0,1:T(8,128)(2,1)} %copy.54) | copy-start | bytes 196612
  54.8 2.8 copy-start.8
  82.0 5.2 %copy-start.11 = (s32[64,8]{0,1:T(8,128)S(1)}, s32[64,8]{0,1:T(8,128)}, u32[]{:S(2)}) copy-start(s32[64,8]{0,1:T(8,128)} %param.31) | copy-start | bytes 6148
  82.0 6.9 %copy-start.14 = (s32[64]{0:T(128)S(1)}, s32[64]{0:T(128)}, u32[]{:S(2)}) copy-start(s32[64]{0:T(128)} %param.33) | copy-start | bytes 772
  82.0 31.2 %copy-start.3 = (bf16[64,2048]{1,0:T(8,128)(2,1)S(1)}, bf16[64,2048]{1,0:T(8,128)(2,1)}, u32[]{:S(2)}) copy-start(bf16[64,2048]{1,0:T(8,128)(2,1)} %param.19) | copy-start | bytes 786436
  82.0 32.4 %copy-start.10 = (f32[2048]{0:T(1024)S(1)}, f32[2048]{0:T(1024)}, u32[]{:S(2)}) copy-start(f32[2048]{0:T(1024)} %param.30) | copy-start | bytes 24580
  82.0 55.9 %all-to-all-start.2 = ((bf16[32,192,256]{2,1,0:T(8,128)(2,1)}), bf16[32,192,256]{2,1,0:T(8,128)(2,1)}, u32[]{:S(2)}, u32[]{:S(2)}) async-start(bf16[32,192,256]{2,1,0:T(8,128)(2,1)} %bitcast.114), calls=%async_computation.3 | async-start | bytes 6291456 | tf_op jit(solution)/shard_map/all_to_all | solution.py:330
  130.1 16.4 %copy-start.15 = (s32[32]{0:T(128)S(1)}, s32[32]{0:T(128)}, u32[]{:S(2)}) copy-start(s32[32]{0:T(128)} %param.34) | copy-start | bytes 388
  137.8 71.3 %all-to-all-start = ((bf16[128,160,128]{2,1,0:T(8,128)(2,1)}), bf16[128,160,128]{2,1,0:T(8,128)(2,1)}, u32[]{:S(2)}, u32[]{:S(2)}) async-start(bf16[128,160,128]{2,1,0:T(8,128)(2,1)} %bitcast_select_fusion), calls=%async_computation.1 | async-start | bytes 10485760 | tf_op jit(solution)/shard_map/all_to_all | solution.py:291
  145.2 18.3 %collective-permute-start = (bf16[3,2048,256]{2,1,0:T(8,128)(2,1)}, bf16[3,2048,256]{2,1,0:T(8,128)(2,1)}, u32[]{:S(2)}, u32[]{:S(2)}) collective-permute-start(bf16[3,2048,256]{2,1,0:T(8,128)(2,1)} %get-tuple-element.24), channel_id=1, source_target_pairs={{0,1},{1,0},{2,3},{3,2},{4,5},{5,4},{6,7},{7,6},{8,9},{9,8},{10,11... | collective-permute-start | bytes 9437192 | tf_op jit(solution)/shard_map/ppermute | solution.py:265
  209.1 46.2 %all-to-all-start.4 = ((bf16[32,192,256]{2,1,0:T(8,128)(2,1)}), bf16[32,192,256]{2,1,0:T(8,128)(2,1)}, u32[]{:S(2)}, u32[]{:S(2)}) async-start(bf16[32,192,256]{2,1,0:T(8,128)(2,1)} %broadcast_select_fusion), calls=%async_computation.5 | async-start | bytes 6291456 | tf_op jit(solution)/shard_map/all_to_all | solution.py:345
  214.0 5.2 %copy-start.4 = (bf16[1,2048,256]{2,1,0:T(8,128)(2,1)S(1)}, bf16[1,2048,256]{2,1,0:T(8,128)(2,1)}, u32[]{:S(2)}) copy-start(bf16[1,2048,256]{2,1,0:T(8,128)(2,1)} %get-tuple-element.28) | copy-start | bytes 3145732
  252.9 11.3 %copy-start.12 = (f32[64,8]{0,1:T(8,128)S(1)}, f32[64,8]{0,1:T(8,128)}, u32[]{:S(2)}) copy-start(f32[64,8]{0,1:T(8,128)} %param.32) | copy-start | bytes 6148
  255.3 72.8 %all-to-all-start.1 = ((bf16[128,160,128]{2,1,0:T(8,128)(2,1)}), bf16[128,160,128]{2,1,0:T(8,128)(2,1)}, u32[]{:S(2)}, u32[]{:S(2)}) async-start(bf16[128,160,128]{2,1,0:T(8,128)(2,1)} %reshape.288), calls=%async_computation.2 | async-start | bytes 10485760 | tf_op jit(solution)/shard_map/all_to_all | solution.py:310
  336.7 5.6 %copy-start.2 = (f32[64,2048]{1,0:T(8,128)S(1)}, f32[64,2048]{1,0:T(8,128)}, u32[]{:S(2)}) copy-start(f32[64,2048]{1,0:T(8,128)} %reduce-scatter.2.cloned.1.call-done) | copy-start | bytes 1572868
  342.3 4.7 %copy-start.1 = (bf16[512,2048]{1,0:T(8,128)(2,1)S(1)}, bf16[512,2048]{1,0:T(8,128)(2,1)}, u32[]{:S(2)}) copy-start(bf16[512,2048]{1,0:T(8,128)(2,1)} %param.29) | copy-start | bytes 6291460
Sparse Core Ops, SparseCore 0:
  61.5 51.5 reduce-scatter.1
